TPU v7x, 32 devices: a whole 2x2x4 slice. The times are simulated.
32 devices in a mesh: tiles: 2 (over y), pat: 16 (over z, x, core).
Axes of the slice: x: 2, y: 2, z: 4, core: 2. Of those that a mesh axis runs over, the one named last changes fastest.
Arguments:
- slab_phase: float32 [6, 1024, 1024], P('tiles', 'pat'), parts along dimension 0, may hold values from -2 to 2
- pupil_phase: float32 [1024, 1024], P('pat'), may hold values from -5 to 5
- pupil_mask: int32 [1024, 1024], P('pat'), may hold values from 0 to 1, as said below
- led_code: int32 [4, 2], replicated, may hold values from 0 to 1, as said below
- led_freq: int32 [2, 2], replicated, may hold values from -32 to 32
- measured: int32 [8, 1024, 1024], P('tiles', 'pat'), parts along dimension 0, may hold values from 1 to 2048
Outputs:
- phase_grad: float32 [6, 1024, 1024], P('tiles', 'pat'), parts along dimension 0
There are 2 independent parts, one for each index of `tiles`. A program takes and returns all parts, laid end to end along the dimension named above; an argument that names none is the same for every part. Nothing has to cross between parts.
Inputs may be any that keep to these rules, and one draw needn't show every extreme that they name: `pupil_mask`: 1 at every frequency pair with freq(u)^2 + freq(v)^2 <= 9216, 0 where it is >= 16384, either value between. `led_code`: pattern p always has LED p mod 2 switched on.
All inputs are finite; a program needn't handle non-finite values.
Results may differ from a plain program's by a relative error of at most 0.0003.
Values sent between devices are 32-bit elements; how exact they have to be, the bound alone decides.
A program may use at most 128 MiB of HBM per device.

v0:
```python
import math

import jax
import jax.numpy as jnp
from jax import lax
from jax.sharding import PartitionSpec as P

spread_rate = 0.3
highest = lax.Precision.HIGHEST


def frequency(grid_index, grid_size):
    return (grid_index + grid_size // 2) % grid_size - grid_size // 2


def complex_times(values, factor):
    real_part = values[0] * factor[0] - values[1] * factor[1]
    imag_part = values[0] * factor[1] + values[1] * factor[0]
    return jnp.stack([real_part, imag_part])


def dft_block(length, direction, norm_factor):
    grid_index = jnp.arange(length, dtype=jnp.int32)
    angles = (grid_index[:, None] * grid_index[None, :] % length).astype(jnp.float32) * (
        2.0 * math.pi / length
    )
    cosine = jnp.cos(angles) * norm_factor
    signed_sine = direction * jnp.sin(angles) * norm_factor
    real_rows = jnp.stack([cosine, signed_sine], 1)
    imag_rows = jnp.stack([-signed_sine, cosine], 1)
    return jnp.stack([real_rows, imag_rows], 0)


def twiddle_table(short_size, long_size, grid_size, direction):
    short_index = jnp.arange(short_size, dtype=jnp.int32)
    long_index = jnp.arange(long_size, dtype=jnp.int32)
    angles = (short_index[:, None] * long_index[None, :] % grid_size).astype(jnp.float32) * (
        2.0 * math.pi / grid_size
    )
    return jnp.stack([jnp.cos(angles), direction * jnp.sin(angles)])


def table_set(col_count, dev_count, grid_size, direction):
    short_table = dft_block(col_count, direction, 1.0)
    long_table = dft_block(dev_count, direction, 1.0 / math.sqrt(grid_size))
    return (short_table, long_table, twiddle_table(col_count, dev_count, grid_size, direction))


def to_fourier(wave_field, tables, dev_count):
    short_table, long_table, twiddles = tables
    led_count = wave_field.shape[1]
    row_count = wave_field.shape[2]
    grid_size = wave_field.shape[3]
    col_count = grid_size // dev_count
    shaped = wave_field.reshape(2, led_count, row_count, col_count, dev_count)
    sectioned = jnp.einsum("zlrmq,zmwc->wlrcq", shaped, short_table, precision=highest)
    sectioned = complex_times(sectioned, twiddles)
    outgoing = jnp.einsum("wlrcq,wqvd->dvlcr", sectioned, long_table, precision=highest)
    incoming = lax.all_to_all(
        outgoing.reshape(dev_count, -1), "pat", split_axis=0, concat_axis=0, tiled=True
    )
    incoming = incoming.reshape(dev_count, 2, led_count, col_count, row_count)
    sectioned = jnp.einsum("swlcr,wsvj->vlcrj", incoming, long_table, precision=highest)
    sectioned = complex_times(sectioned, twiddles)
    sectioned = jnp.einsum("wlcrj,wrvh->vlchj", sectioned, short_table, precision=highest)
    return sectioned.reshape(2, led_count, col_count, grid_size)


def to_space(spectrum, tables, dev_count):
    short_table, long_table, twiddles = tables
    led_count = spectrum.shape[1]
    col_count = spectrum.shape[2]
    grid_size = spectrum.shape[3]
    row_count = grid_size // dev_count
    shaped = spectrum.reshape(2, led_count, col_count, row_count, dev_count)
    sectioned = jnp.einsum("zlcmq,zmwr->wlcrq", shaped, short_table, precision=highest)
    sectioned = complex_times(sectioned, twiddles)
    outgoing = jnp.einsum("wlcrq,wqvd->dvlcr", sectioned, long_table, precision=highest)
    incoming = lax.all_to_all(
        outgoing.reshape(dev_count, -1), "pat", split_axis=0, concat_axis=0, tiled=True
    )
    incoming = incoming.reshape(dev_count, 2, led_count, col_count, row_count)
    sectioned = jnp.einsum("swlcr,wsvj->vlrcj", incoming, long_table, precision=highest)
    sectioned = complex_times(sectioned, twiddles)
    sectioned = jnp.einsum("wlrcj,wcvh->vlrhj", sectioned, short_table, precision=highest)
    return sectioned.reshape(2, led_count, row_count, grid_size)


def body(slab_phase, pupil_phase, pupil_mask, led_code, led_freq, measured):
    dev_count = lax.axis_size("pat")
    position = lax.axis_index("pat")
    slab_count, row_count, grid_size = slab_phase.shape
    col_count = grid_size // dev_count
    pattern_count, led_count = led_code.shape
    area = float(grid_size * grid_size)
    forward_set = table_set(col_count, dev_count, grid_size, -1.0)
    inverse_set = table_set(col_count, dev_count, grid_size, 1.0)
    conjugate = jnp.array([1.0, -1.0], jnp.float32)[:, None, None]
    col_freq = frequency(position * col_count + jnp.arange(col_count, dtype=jnp.int32), grid_size)
    row_freq = frequency(jnp.arange(grid_size, dtype=jnp.int32), grid_size)
    radius = col_freq[:, None] * col_freq[:, None] + row_freq[None, :] * row_freq[None, :]
    cutoff = grid_size // 2 * (grid_size // 2)
    inside = radius <= cutoff
    height = jnp.sqrt(jnp.maximum(cutoff - radius, 0).astype(jnp.float32))
    phase_shift = spread_rate * (height - grid_size // 2)
    propagator = jnp.stack(
        [jnp.where(inside, jnp.cos(phase_shift), 0.0), jnp.where(inside, jnp.sin(phase_shift), 0.0)]
    )
    opening = pupil_mask.astype(jnp.float32)
    pupil = jnp.stack([opening * jnp.cos(pupil_phase), opening * jnp.sin(pupil_phase)])
    propagator_conj = propagator * conjugate
    pupil_conj = pupil * conjugate
    row_index = position * row_count + jnp.arange(row_count, dtype=jnp.int32)
    col_index = jnp.arange(grid_size, dtype=jnp.int32)
    tilt_index = (
        led_freq[:, 0][:, None, None] * row_index[None, :, None]
        + led_freq[:, 1][:, None, None] * col_index[None, None, :]
    ) % grid_size
    tilt_angle = tilt_index.astype(jnp.float32) * (2.0 * math.pi / grid_size)
    illumination = jnp.stack([jnp.cos(tilt_angle), jnp.sin(tilt_angle)])
    transmission = jnp.stack([jnp.cos(slab_phase), jnp.sin(slab_phase)])
    group_count = 1
    group_size = led_count // group_count
    wave_groups = [illumination]
    passed_groups = []
    for slab_index in range(slab_count):
        factor = transmission[:, slab_index]
        passed = [complex_times(wave_field, factor) for wave_field in wave_groups]
        passed_groups.append(passed)
        spectral_factor = propagator if slab_index < slab_count - 1 else pupil
        wave_groups = [
            to_space(
                complex_times(to_fourier(passed_field, forward_set, dev_count), spectral_factor),
                inverse_set,
                dev_count,
            )
            for passed_field in passed
        ]
    camera = wave_groups[0]
    led_power = camera[0] * camera[0] + camera[1] * camera[1]
    code_float = led_code.astype(jnp.float32)
    pattern_power = jnp.dot(
        code_float, led_power.reshape(led_count, -1), precision=highest
    ).reshape(pattern_count, row_count, grid_size)
    counts = measured.astype(jnp.float32)
    power_sum, count_sum = lax.psum(
        (jnp.sum(pattern_power, axis=(1, 2)), jnp.sum(counts, axis=(1, 2))), "pat"
    )
    mean_power = power_sum / area
    mean_count = count_sum / area
    relative = pattern_power / mean_power[:, None, None]
    misfit = relative - counts / mean_count[:, None, None]
    coupling = lax.psum(jnp.sum(misfit * relative, axis=(1, 2)), "pat") / area
    pattern_weight = (misfit - coupling[:, None, None]) / mean_power[:, None, None]
    led_weight = jnp.dot(
        code_float.T, pattern_weight.reshape(pattern_count, -1), precision=highest
    ).reshape(led_count, row_count, grid_size)
    camera_adjoint = 2.0 * led_weight[None] * camera
    adjoint_groups = [camera_adjoint]
    gradients = [None] * slab_count
    for slab_index in range(slab_count - 1, -1, -1):
        spectral_factor = pupil_conj if slab_index == slab_count - 1 else propagator_conj
        back_groups = [
            to_space(
                complex_times(to_fourier(adjoint_field, forward_set, dev_count), spectral_factor),
                inverse_set,
                dev_count,
            )
            for adjoint_field in adjoint_groups
        ]
        gradient = jnp.zeros((row_count, grid_size), jnp.float32)
        for passed_field, back_field in zip(passed_groups[slab_index], back_groups):
            gradient = jnp.sum(
                passed_field[0] * back_field[1] - passed_field[1] * back_field[0], axis=0
            )
        gradients[slab_index] = gradient
        if slab_index > 0:
            release = transmission[:, slab_index] * conjugate
            adjoint_groups = [complex_times(back_field, release) for back_field in back_groups]
    return jnp.stack(gradients)


def solution(mesh):
    in_specs = (
        P("tiles", "pat", None),
        P("pat", None),
        P("pat", None),
        P(),
        P(),
        P("tiles", "pat", None),
    )
    out_specs = P("tiles", "pat", None)
    return jax.shard_map(body, mesh=mesh, in_specs=in_specs, out_specs=out_specs, check_vma=False)
```

profile of v0, /device:TPU:0, one launch (start us, length us, event | category | flops | bytes accessed | tf_op | source)
XLA Modules:
  0.0 786.0 jit_solution(7634403224330466564)
XLA Ops:
  3.3 5.5 cosine_bitcast_fusion
  32.3 7.4 all-to-all-start
  42.0 20.6 %all-to-all-done = f32[16,1,16384]{2,1,0:T(1,128)S(1)} async-done(((f32[16,1,16384]{2,1,0:T(1,128)}), f32[16,1,16384]{2,1,0:T(1,128)S(1)}, u32[]{:S(2)}, u32[]{:S(2)}) %all-to-all-start) | async-done | bytes 1048608 | tf_op jit(solution)/shard_map/all_to_all | solution.py:59
  90.0 7.1 all-to-all-start.1
  99.0 20.8 %all-to-all-done.1 = f32[16,1,16384]{2,1,0:T(1,128)S(1)} async-done(((f32[16,1,16384]{2,1,0:T(1,128)}), f32[16,1,16384]{2,1,0:T(1,128)S(1)}, u32[]{:S(2)}, u32[]{:S(2)}) %all-to-all-start.1) | async-done | bytes 1048608 | tf_op jit(solution)/shard_map/all_to_all | solution.py:79
  145.9 31.3 %all_to_all.120 = f32[16,1,16384]{2,1,0:T(1,128)S(1)} all-to-all(f32[16,1,16384]{2,1,0:T(1,128)S(1)} %all_to_all.98), channel_id=1, replica_groups=mesh['tiles'=2,'pat'=16] {'pat'}, dimensions={0} | all-to-all | bytes 2097152 | tf_op jit(solution)/shard_map/all_to_all | solution.py:59
  211.8 20.8 %all-to-all-done.3 = f32[16,1,16384]{2,1,0:T(1,128)S(1)} async-done(((f32[16,1,16384]{2,1,0:T(1,128)}), f32[16,1,16384]{2,1,0:T(1,128)S(1)}, u32[]{:S(2)}, u32[]{:S(2)}) %all-to-all-start.3) | async-done | bytes 1048608 | tf_op jit(solution)/shard_map/all_to_all | solution.py:79
  257.0 6.9 all-to-all-start.4
  269.1 17.8 %all-to-all-done.4 = f32[16,1,16384]{2,1,0:T(1,128)S(1)} async-done(((f32[16,1,16384]{2,1,0:T(1,128)}), f32[16,1,16384]{2,1,0:T(1,128)S(1)}, u32[]{:S(2)}, u32[]{:S(2)}) %all-to-all-start.4) | async-done | bytes 1048608 | tf_op jit(solution)/shard_map/all_to_all | solution.py:59
  311.8 7.0 all-to-all-start.5
  319.0 22.7 %all-to-all-done.5 = f32[16,1,16384]{2,1,0:T(1,128)S(1)} async-done(((f32[16,1,16384]{2,1,0:T(1,128)}), f32[16,1,16384]{2,1,0:T(1,128)S(1)}, u32[]{:S(2)}, u32[]{:S(2)}) %all-to-all-start.5) | async-done | bytes 1048608 | tf_op jit(solution)/shard_map/all_to_all | solution.py:79
  354.8 5.4 copy.290
  369.5 34.9 %all-reduce = (f32[4]{0:T(128)S(1)}, f32[4]{0:T(128)S(1)}) all-reduce(f32[4]{0:T(128)S(1)} %convert_reduce_fusion, f32[4]{0:T(128)S(1)} %get-tuple-element.115), channel_id=1, replica_groups=mesh['tiles'=2,'pat'=16] {'pat'}, use_global_device_ids=true, to_apply=%region_3.4 | all-reduce | flops 8 | bytes 64 | tf_op jit(solution)/shard_map/psum | solution.py:146
  406.4 29.9 %psum.23 = f32[4]{0:T(128)S(1)} all-reduce(f32[4]{0:T(128)S(1)} %multiply_reduce_fusion), channel_id=1, replica_groups=mesh['tiles'=2,'pat'=16] {'pat'}, use_global_device_ids=true, to_apply=%region_5.6 | all-reduce | flops 4 | bytes 32 | tf_op jit(solution)/shard_map/psum | solution.py:153
  474.5 15.6 %all-to-all-done.6 = f32[16,1,16384]{2,1,0:T(1,128)} async-done(((f32[16,1,16384]{2,1,0:T(1,128)}), f32[16,1,16384]{2,1,0:T(1,128)}, u32[]{:S(2)}, u32[]{:S(2)}) %all-to-all-start.6) | async-done | bytes 1048608 | tf_op jit(solution)/shard_map/all_to_all | solution.py:59
  516.1 7.1 all-to-all-start.7
  525.3 20.5 %all-to-all-done.7 = f32[16,1,16384]{2,1,0:T(1,128)S(1)} async-done(((f32[16,1,16384]{2,1,0:T(1,128)}), f32[16,1,16384]{2,1,0:T(1,128)S(1)}, u32[]{:S(2)}, u32[]{:S(2)}) %all-to-all-start.7) | async-done | bytes 1048608 | tf_op jit(solution)/shard_map/all_to_all | solution.py:79
  571.4 6.8 all-to-all-start.8
  578.7 22.4 %all-to-all-done.8 = f32[16,1,16384]{2,1,0:T(1,128)S(1)} async-done(((f32[16,1,16384]{2,1,0:T(1,128)}), f32[16,1,16384]{2,1,0:T(1,128)S(1)}, u32[]{:S(2)}, u32[]{:S(2)}) %all-to-all-start.8) | async-done | bytes 1048608 | tf_op jit(solution)/shard_map/all_to_all | solution.py:59
  628.3 7.3 all-to-all-start.9
  637.6 20.5 %all-to-all-done.9 = f32[16,1,16384]{2,1,0:T(1,128)S(1)} async-done(((f32[16,1,16384]{2,1,0:T(1,128)}), f32[16,1,16384]{2,1,0:T(1,128)S(1)}, u32[]{:S(2)}, u32[]{:S(2)}) %all-to-all-start.9) | async-done | bytes 1048608 | tf_op jit(solution)/shard_map/all_to_all | solution.py:79
  685.5 31.3 %all_to_all.121 = f32[16,1,16384]{2,1,0:T(1,128)S(1)} all-to-all(f32[16,1,16384]{2,1,0:T(1,128)S(1)} %all_to_all.106), channel_id=1, replica_groups=mesh['tiles'=2,'pat'=16] {'pat'}, dimensions={0} | all-to-all | bytes 2097152 | tf_op jit(solution)/shard_map/all_to_all | solution.py:59
  743.8 5.4 all-to-all-start.11
  751.5 20.4 %all-to-all-done.11 = f32[16,1,16384]{2,1,0:T(1,128)S(1)} async-done(((f32[16,1,16384]{2,1,0:T(1,128)}), f32[16,1,16384]{2,1,0:T(1,128)S(1)}, u32[]{:S(2)}, u32[]{:S(2)}) %all-to-all-start.11) | async-done | bytes 1048608 | tf_op jit(solution)/shard_map/all_to_all | solution.py:79
  (325 shorter events, 388.5 us)
Async XLA Ops:
  32.3 30.3 %all-to-all-start = ((f32[16,1,16384]{2,1,0:T(1,128)}), f32[16,1,16384]{2,1,0:T(1,128)S(1)}, u32[]{:S(2)}, u32[]{:S(2)}) async-start(f32[16,1,16384]{2,1,0:T(1,128)} %all_to_all.96), calls=%async_computation | async-start | bytes 2097152 | tf_op jit(solution)/shard_map/all_to_all | solution.py:59
  90.0 7.1 copy-start.25
  90.0 8.1 %copy-start.24 = (f32[1,1,64,1024]{2,3,1,0:T(8,128)S(1)}, f32[1,1,64,1024]{2,3,1,0:T(8,128)}, u32[]{:S(2)}) copy-start(f32[1,1,64,1024]{2,3,1,0:T(8,128)} %get-tuple-element.118) | copy-start | bytes 786436
  90.0 29.8 %all-to-all-start.1 = ((f32[16,1,16384]{2,1,0:T(1,128)}), f32[16,1,16384]{2,1,0:T(1,128)S(1)}, u32[]{:S(2)}, u32[]{:S(2)}) async-start(f32[16,1,16384]{2,1,0:T(1,128)} %all_to_all.97), calls=%async_computation.1 | async-start | bytes 2097152 | tf_op jit(solution)/shard_map/all_to_all | solution.py:79
  202.2 7.7 copy-start.23
  204.5 28.1 %all-to-all-start.3 = ((f32[16,1,16384]{2,1,0:T(1,128)}), f32[16,1,16384]{2,1,0:T(1,128)S(1)}, u32[]{:S(2)}, u32[]{:S(2)}) async-start(f32[16,1,16384]{2,1,0:T(1,128)} %all_to_all.99), calls=%async_computation.3 | async-start | bytes 2097152 | tf_op jit(solution)/shard_map/all_to_all | solution.py:79
  253.6 10.4 %copy-start.42 = (f32[64,1024]{1,0:T(8,128)S(1)}, f32[64,1024]{1,0:T(8,128)}, u32[]{:S(2)}) copy-start(f32[64,1024]{1,0:T(8,128)} %param.8) | copy-start | bytes 786436
  257.0 7.1 copy-start.43
  257.0 29.8 %all-to-all-start.4 = ((f32[16,1,16384]{2,1,0:T(1,128)}), f32[16,1,16384]{2,1,0:T(1,128)S(1)}, u32[]{:S(2)}, u32[]{:S(2)}) async-start(f32[16,1,16384]{2,1,0:T(1,128)} %all_to_all.100), calls=%async_computation.4 | async-start | bytes 2097152 | tf_op jit(solution)/shard_map/all_to_all | solution.py:59
  309.5 9.3 %copy-start.12 = (s32[4,64,1024]{2,1,0:T(8,128)S(1)}, s32[4,64,1024]{2,1,0:T(8,128)}, u32[]{:S(2)}) copy-start(s32[4,64,1024]{2,1,0:T(8,128)} %param.12) | copy-start | bytes 3145732
  311.8 29.8 %all-to-all-start.5 = ((f32[16,1,16384]{2,1,0:T(1,128)}), f32[16,1,16384]{2,1,0:T(1,128)S(1)}, u32[]{:S(2)}, u32[]{:S(2)}) async-start(f32[16,1,16384]{2,1,0:T(1,128)} %all_to_all.101), calls=%async_computation.5 | async-start | bytes 2097152 | tf_op jit(solution)/shard_map/all_to_all | solution.py:79
  462.6 6.8 copy-start.1
  462.6 6.8 copy-start.3
  462.6 6.8 copy-start.45
  462.6 27.5 %all-to-all-start.6 = ((f32[16,1,16384]{2,1,0:T(1,128)}), f32[16,1,16384]{2,1,0:T(1,128)}, u32[]{:S(2)}, u32[]{:S(2)}) async-start(f32[16,1,16384]{2,1,0:T(1,128)} %all_to_all.102), calls=%async_computation.6 | async-start | bytes 2097152 | tf_op jit(solution)/shard_map/all_to_all | solution.py:59
  513.8 9.5 %copy-start.21 = (f32[2,64,1024]{1,2,0:T(8,128)S(1)}, f32[2,64,1024]{1,2,0:T(8,128)}, u32[]{:S(2)}) copy-start(f32[2,64,1024]{1,2,0:T(8,128)} %get-tuple-element.10) | copy-start | bytes 1572868
  516.1 29.6 %all-to-all-start.7 = ((f32[16,1,16384]{2,1,0:T(1,128)}), f32[16,1,16384]{2,1,0:T(1,128)S(1)}, u32[]{:S(2)}, u32[]{:S(2)}) async-start(f32[16,1,16384]{2,1,0:T(1,128)} %all_to_all.103), calls=%async_computation.7 | async-start | bytes 2097152 | tf_op jit(solution)/shard_map/all_to_all | solution.py:79
  567.9 10.3 %copy-start.20 = (f32[2,64,1024]{1,2,0:T(8,128)S(1)}, f32[2,64,1024]{1,2,0:T(8,128)}, u32[]{:S(2)}) copy-start(f32[2,64,1024]{1,2,0:T(8,128)} %get-tuple-element.113) | copy-start | bytes 1572868
  571.4 29.7 %all-to-all-start.8 = ((f32[16,1,16384]{2,1,0:T(1,128)}), f32[16,1,16384]{2,1,0:T(1,128)S(1)}, u32[]{:S(2)}, u32[]{:S(2)}) async-start(f32[16,1,16384]{2,1,0:T(1,128)} %all_to_all.104), calls=%async_computation.8 | async-start | bytes 2097152 | tf_op jit(solution)/shard_map/all_to_all | solution.py:59
  628.3 7.3 copy-start.19
  628.3 29.8 %all-to-all-start.9 = ((f32[16,1,16384]{2,1,0:T(1,128)}), f32[16,1,16384]{2,1,0:T(1,128)S(1)}, u32[]{:S(2)}, u32[]{:S(2)}) async-start(f32[16,1,16384]{2,1,0:T(1,128)} %all_to_all.105), calls=%async_computation.9 | async-start | bytes 2097152 | tf_op jit(solution)/shard_map/all_to_all | solution.py:79
  741.5 7.7 copy-start.36
  743.8 6.5 copy-start.37
  743.8 28.1 %all-to-all-start.11 = ((f32[16,1,16384]{2,1,0:T(1,128)}), f32[16,1,16384]{2,1,0:T(1,128)S(1)}, u32[]{:S(2)}, u32[]{:S(2)}) async-start(f32[16,1,16384]{2,1,0:T(1,128)} %all_to_all.107), calls=%async_computation.11 | async-start | bytes 2097152 | tf_op jit(solution)/shard_map/all_to_all | solution.py:79
  (32 other events, 74.7 us)
where the time goes:
time: 798 us; the launch traced here: 786 us
  waiting for transfers between devices  202 us (25%)
  local copies, waits for them, and re-layouts  164 us (21%)
  matrix products  142 us (18%)
  blocking collectives  127 us (16%)
  other arithmetic  83.2 us (10%)
  starting transfers between devices  65 us (8%)
    all_to_all x6, waiting for transfers between devices, to_space(): lax.all_to_all(outgoing.reshape(dev_count, -1), 'pat', split_axis=0, conc...  126 us
    all_to_all x4, waiting for transfers between devices, to_fourier(): lax.all_to_all(outgoing.reshape(dev_count, -1), 'pat', split_axis=0, conc...  76.4 us
    all_to_all x2, blocking collectives, to_fourier(): lax.all_to_all(outgoing.reshape(dev_count, -1), 'pat', split_axis=0, conc...  62.5 us
    all_to_all x6, starting transfers between devices, to_space(): lax.all_to_all(outgoing.reshape(dev_count, -1), 'pat', split_axis=0, conc...  39.3 us
    psum x1, blocking collectives, body(): lax.psum((jnp.sum(pattern_power, axis=(1, 2)), jnp.sum(counts, axis=(1, 2...  34.9 us
    another operation x12, local copies, waits for them, and re-layouts, complex_times(): return jnp.stack([real_part, imag_part])  33.1 us
    psum x1, blocking collectives, body(): coupling = lax.psum(jnp.sum(misfit * relative, axis=(1, 2)), 'pat') / area  29.9 us
    dot_general x6, matrix products, to_fourier(): jnp.einsum('swlcr,wsvj->vlcrj', incoming, long_table, precision=highest)  26 us
  transfers between devices with their start and end apart: 10, of which 10 were waited for; matrix products, arithmetic and copies ran while one was open for 3% of the time, Pallas kernels for 0%

commit v1 on v0

--- a/solution.py
+++ b/solution.py
@@ -1,8 +1,13 @@
+import functools
 import math
+import types
 
 import jax
 import jax.numpy as jnp
+import numpy as np
 from jax import lax
+from jax.experimental import pallas as pl
+from jax.experimental.pallas import tpu as pltpu
 from jax.sharding import PartitionSpec as P
 
 spread_rate = 0.3
@@ -86,7 +91,7 @@
     return sectioned.reshape(2, led_count, row_count, grid_size)
 
 
-def body(slab_phase, pupil_phase, pupil_mask, led_code, led_freq, measured):
+def plain_body(slab_phase, pupil_phase, pupil_mask, led_code, led_freq, measured):
     dev_count = lax.axis_size("pat")
     position = lax.axis_index("pat")
     slab_count, row_count, grid_size = slab_phase.shape
@@ -180,6 +185,563 @@
     return jnp.stack(gradients)
 
 
+class Names(types.SimpleNamespace):
+    pass
+
+
+pupil_radius = 128
+lanes = 128
+f32 = jnp.float32
+bf16 = jnp.bfloat16
+
+
+def halves(table):
+    table32 = np.asarray(table, np.float32)
+    high = table32.astype(bf16)
+    low = (table32 - high.astype(np.float32)).astype(bf16)
+    return np.stack([high, low])
+
+
+def row_tables(size, block, band_block):
+    quarter = size // 4
+    pos = np.arange(quarter)
+    angle = 2.0 * np.pi * ((pos[:, None] * pos[None, :]) % quarter) / quarter
+    cosine = np.cos(angle) / math.sqrt(size)
+    sine = np.sin(angle) / math.sqrt(size)
+
+    def forward(freqs, width):
+        parts = []
+        for first in range(0, len(freqs), width):
+            pick = freqs[first : first + width] % quarter
+            left = np.concatenate([cosine[:, pick], sine[:, pick]], 0)
+            right = np.concatenate([-sine[:, pick], cosine[:, pick]], 0)
+            parts.append(np.concatenate([left, right], 1))
+        return np.concatenate(parts, 1)
+
+    full = forward(pos, block)
+    reach = pupil_radius // 4
+    band = forward(np.arange(-reach, reach), band_block)
+    theta = 2.0 * np.pi * (np.arange(4)[:, None] * pos[None, :]) / size
+    twiddle = np.concatenate([np.cos(theta), np.sin(theta)], 0).astype(np.float32)
+    return Names(
+        full=jnp.asarray(halves(full)),
+        full_inv=jnp.asarray(halves(full.T)),
+        band=jnp.asarray(halves(band)),
+        band_inv=jnp.asarray(halves(band.T)),
+        twiddle=jnp.asarray(twiddle),
+    )
+
+
+def col_tables(size):
+    quarter = size // 4
+    pos = np.arange(quarter)
+    angle = 2.0 * np.pi * ((pos[:, None] * pos[None, :]) % quarter) / quarter
+    both = np.concatenate([np.cos(angle), np.sin(angle)], 0) / math.sqrt(size)
+    theta = 2.0 * np.pi * (np.arange(1, 4)[:, None] * pos[None, :]) / size
+    twiddle = np.stack([np.cos(theta), np.sin(theta)]).astype(np.float32)
+    twiddle = np.ascontiguousarray(np.broadcast_to(twiddle[..., None], twiddle.shape + (lanes,)))
+    freqs = np.arange(-pupil_radius, pupil_radius)
+    angle = 2.0 * np.pi * ((np.arange(size)[:, None] * freqs[None, :]) % size) / size
+    cosine = np.cos(angle) / math.sqrt(size)
+    sine = np.sin(angle) / math.sqrt(size)
+    band = halves(np.concatenate([cosine, sine], 1))
+    band_inv = halves(np.concatenate([cosine.T, sine.T], 1))
+    return Names(both=halves(both), twiddle=twiddle, band=band, band_inv=band_inv)
+
+
+def split(value):
+    high = value.astype(bf16)
+    return high, (value - high.astype(f32)).astype(bf16)
+
+
+def dot3(left, right):
+    def dot(a, b):
+        return jnp.dot(a, b, preferred_element_type=f32)
+
+    return dot(left[0], right[0]) + (dot(left[0], right[1]) + dot(left[1], right[0]))
+
+
+def turn(value):
+    rolled = pltpu.roll(value, lanes // 2, 1)
+    lane = lax.broadcasted_iota(jnp.int32, value.shape, 1)
+    return jnp.where(lane < lanes // 2, rolled, -rolled)
+
+
+def row_spread(blocks, twiddle_ref):
+    (r0, i0), (r1, i1), (r2, i2), (r3, i3) = blocks
+    sr, si, tr, ti = r0 + r2, i0 + i2, r1 + r3, i1 + i3
+    dr, di, er, ei = r0 - r2, i0 - i2, r1 - r3, i1 - i3
+    mixed = [(sr + tr, si + ti), (dr + ei, di - er), (sr - tr, si - ti), (dr - ei, di + er)]
+    out = [mixed[0]]
+    for j in range(1, 4):
+        cosine, sine = twiddle_ref[j : j + 1, :], twiddle_ref[4 + j : 5 + j, :]
+        re, im = mixed[j]
+        out.append((re * cosine + im * sine, im * cosine - re * sine))
+    return out
+
+
+def row_gather(parts, twiddle_ref):
+    g = [parts[0]]
+    for j in range(1, 4):
+        cosine, sine = twiddle_ref[j : j + 1, :], twiddle_ref[4 + j : 5 + j, :]
+        re, im = parts[j]
+        g.append((re * cosine - im * sine, im * cosine + re * sine))
+    (r0, i0), (r1, i1), (r2, i2), (r3, i3) = g
+    sr, si, tr, ti = r0 + r2, i0 + i2, r1 + r3, i1 + i3
+    dr, di, er, ei = r0 - r2, i0 - i2, r1 - r3, i1 - i3
+    return [(sr + tr, si + ti), (dr - ei, di + er), (sr - tr, si - ti), (dr + ei, di - er)]
+
+
+def row_kernel(spec, *refs):
+    ref = Names(**dict(zip(spec.names, refs)))
+    count, rows, quarter = spec.count, spec.rows, spec.quarter
+    devs = spec.devs
+    per = devs // 4
+    step = 16
+    total = count * rows
+    hi, lo, zs, twiddle = ref.hi, ref.lo, ref.zs, ref.twiddle
+    source = spec.source
+    if source == "full":
+        for j in range(4):
+            for q in range(per):
+                block = ref.x[per * j + q].reshape(total, lanes)
+                high, low = split(block)
+                hi[j, :total, q * lanes : (q + 1) * lanes] = high
+                lo[j, :total, q * lanes : (q + 1) * lanes] = low
+        for j in range(4):
+            left = (hi[j, :total, :], lo[j, :total, :])
+            zs[j, :total, :] = dot3(left, (ref.inv[0], ref.inv[1]))
+    elif source == "band":
+        for j in range(4):
+            block = ref.x[per * j : per * (j + 1)].reshape(-1, total)
+            zs[j, :total, :] = dot3(split(block.T), (ref.inv[0], ref.inv[1]))
+    kind = spec.kind
+    if kind == "stats":
+        stats = [jnp.zeros((8, lanes), f32) for _ in range(spec.stat_rows)]
+    if kind == "weigh":
+        sums = jnp.sum(ref.stats[...], 0)
+        sums = jnp.sum(sums, 1, keepdims=True)
+        code = [[ref.code[p, l].astype(f32) for l in range(count)] for p in range(spec.patterns)]
+        area = spec.area
+        power_mean, count_mean, couple = [], [], []
+        base = count + count * (count + 1) // 2
+        for p in range(spec.patterns):
+            mean = sum(sums[l : l + 1] * code[p][l] for l in range(count)) / area
+            mean_count = sums[base + spec.patterns * count + p :][:1] / area
+            square = 0.0
+            at = count
+            for l in range(count):
+                for m in range(l, count):
+                    factor = 1.0 if l == m else 2.0
+                    square = square + (factor * code[p][l] * code[p][m]) * sums[at : at + 1]
+                    at += 1
+            cross = sum(code[p][l] * sums[base + p * count + l :][:1] for l in range(count))
+            power_mean.append(mean)
+            count_mean.append(mean_count)
+            couple.append((square / mean / mean - cross / mean_count / mean) / area)
+
+    def fold(value):
+        total_rows = value[:8]
+        for k in range(1, value.shape[0] // 8):
+            total_rows = total_rows + value[8 * k : 8 * k + 8]
+        out = total_rows[:, :lanes]
+        for k in range(1, value.shape[1] // lanes):
+            out = out + total_rows[:, lanes * k : lanes * (k + 1)]
+        return out
+
+    def chunk(i, carry):
+        base_row = pl.multiple_of(i * step, step)
+        here = pl.ds(base_row, step)
+        fields = []
+        for l in range(count):
+            at = pl.ds(pl.multiple_of(l * rows + base_row, step), step)
+            if source in ("full", "band"):
+                parts = [(zs[j, at, :quarter], zs[j, at, quarter:]) for j in range(4)]
+                fields.append(row_gather(parts, twiddle))
+        cut = [slice(a * quarter, (a + 1) * quarter) for a in range(4)]
+
+        def tilt(l, a, value, sign):
+            rc, rs = ref.tilt_r[2 * l, here, :], ref.tilt_r[2 * l + 1, here, :]
+            cc, cs = ref.tilt_c[2 * l : 2 * l + 1, cut[a]], ref.tilt_c[2 * l + 1 : 2 * l + 2, cut[a]]
+            wide = jnp.concatenate([rc] * (quarter // lanes), 1), jnp.concatenate([rs] * (quarter // lanes), 1)
+            er = wide[0] * cc - wide[1] * cs
+            ei = sign * (wide[0] * cs + wide[1] * cc)
+            re, im = value
+            return re * er - im * ei, re * ei + im * er
+
+        outgoing = []
+        if kind == "enter":
+            outgoing = [[(ref.tr[0, here, c], ref.tr[1, here, c]) for c in cut]]
+        elif kind == "forward" or kind == "forward_band":
+            for l in range(count):
+                at = pl.ds(pl.multiple_of(l * rows + base_row, step), step)
+                blocks = []
+                for a, c in enumerate(cut):
+                    tr, ti = ref.tr[0, here, c], ref.tr[1, here, c]
+                    re, im = fields[l][a]
+                    re, im = re * tr - im * ti, re * ti + im * tr
+                    ref.passed[0, at, c] = re
+                    ref.passed[1, at, c] = im
+                    blocks.append((re, im) if kind == "forward" else tilt(l, a, (re, im), 1.0))
+                outgoing.append(blocks)
+        elif kind == "stats":
+            adds = [0.0] * spec.stat_rows
+            for a, c in enumerate(cut):
+                power = []
+                for l in range(count):
+                    at = pl.ds(pl.multiple_of(l * rows + base_row, step), step)
+                    re, im = fields[l][a]
+                    ref.passed[0, at, c] = re
+                    ref.passed[1, at, c] = im
+                    power.append(re * re + im * im)
+                values = list(power)
+                for l in range(count):
+                    for m in range(l, count):
+                        values.append(power[l] * power[m])
+                seen = [ref.measured[p, here, c].astype(f32) for p in range(spec.patterns)]
+                for p in range(spec.patterns):
+                    for l in range(count):
+                        values.append(seen[p] * power[l])
+                values += seen
+                for k, value in enumerate(values):
+                    adds[k] = adds[k] + fold(value)
+            return tuple(x + y for x, y in zip(carry, adds))
+        elif kind == "weigh":
+            outgoing = [[] for _ in range(count)]
+            for a, c in enumerate(cut):
+                camera, power = [], []
+                for l in range(count):
+                    at = pl.ds(pl.multiple_of(l * rows + base_row, step), step)
+                    re, im = ref.passed[0, at, c], ref.passed[1, at, c]
+                    camera.append((re, im))
+                    power.append(re * re + im * im)
+                weight = [0.0] * count
+                for p in range(spec.patterns):
+                    lit = sum(code[p][l] * power[l] for l in range(count))
+                    seen = ref.measured[p, here, c].astype(f32)
+                    misfit = lit * (1.0 / power_mean[p]) - seen * (1.0 / count_mean[p])
+                    pull = (misfit - couple[p]) * (1.0 / power_mean[p])
+                    for l in range(count):
+                        weight[l] = weight[l] + code[p][l] * pull
+                for l in range(count):
+                    scale = 2.0 * weight[l]
+                    outgoing[l].append((scale * camera[l][0], scale * camera[l][1]))
+        elif kind == "back" or kind == "back_band":
+            grads = [0.0] * 4
+            for l in range(count):
+                at = pl.ds(pl.multiple_of(l * rows + base_row, step), step)
+                blocks = []
+                for a, c in enumerate(cut):
+                    re, im = fields[l][a]
+                    if kind == "back_band":
+                        re, im = tilt(l, a, (re, im), -1.0)
+                    pr, pi = ref.passed[0, at, c], ref.passed[1, at, c]
+                    grads[a] = grads[a] + (pr * im - pi * re)
+                    tr, ti = ref.tr[0, here, c], ref.tr[1, here, c]
+                    blocks.append((re * tr + im * ti, im * tr - re * ti))
+                outgoing.append(blocks)
+            for a, c in enumerate(cut):
+                ref.grad[here, c] = grads[a]
+        elif kind == "leave":
+            for a, c in enumerate(cut):
+                tr, ti = ref.tr[0, here, c], ref.tr[1, here, c]
+                re, im = fields[0][a]
+                ref.grad[here, c] = tr * im - ti * re
+        for l, blocks in enumerate(outgoing):
+            at = pl.ds(pl.multiple_of(l * rows + base_row, step), step)
+            for j, (re, im) in enumerate(row_spread(blocks, twiddle)):
+                high, low = split(re)
+                hi[j, at, :quarter] = high
+                lo[j, at, :quarter] = low
+                high, low = split(im)
+                hi[j, at, quarter:] = high
+                lo[j, at, quarter:] = low
+        return carry
+
+    if kind == "stats":
+        stats = lax.fori_loop(0, rows // step, chunk, tuple(stats))
+        packed = [jnp.sum(row, 0, keepdims=True) for row in stats]
+        packed.append(jnp.zeros((ref.sums.shape[1] - len(packed), lanes), f32))
+        packed = jnp.concatenate(packed, 0)
+        for d in range(devs):
+            ref.sums[d] = packed
+        return
+    lax.fori_loop(0, rows // step, chunk, 0)
+    if spec.target == "full":
+        for j in range(4):
+            y = dot3((hi[j, :total, :], lo[j, :total, :]), (ref.fwd[0], ref.fwd[1]))
+            for q in range(per):
+                ref.y[per * j + q] = y[:, q * lanes : (q + 1) * lanes].reshape(count, rows, lanes)
+    elif spec.target == "band":
+        for j in range(4):
+            y = dot3((hi[j, :total, :], lo[j, :total, :]), (ref.fwd[0], ref.fwd[1]))
+            ref.y[per * j : per * (j + 1)] = y.T.reshape(per, -1, total)
+
+
+def run_rows(kind, source, target, dims, inputs, outputs):
+    spec = Names(**vars(dims), kind=kind, source=source, target=target)
+    count = spec.count
+    total = count * spec.rows
+    wide = 2 * spec.quarter
+    names = list(inputs) + list(outputs) + ["hi", "lo", "zs"]
+    spec.names = names
+    vmem = pl.BlockSpec(memory_space=pltpu.VMEM)
+    in_specs = [
+        pl.BlockSpec(memory_space=pltpu.SMEM) if name == "code" else vmem for name in inputs
+    ]
+    return pl.pallas_call(
+        functools.partial(row_kernel, spec),
+        out_shape=[jax.ShapeDtypeStruct(shape, f32) for shape in outputs.values()],
+        in_specs=in_specs,
+        out_specs=[vmem] * len(outputs),
+        scratch_shapes=[
+            pltpu.VMEM((4, total, wide), bf16),
+            pltpu.VMEM((4, total, wide), bf16),
+            pltpu.VMEM((4, total, wide), f32),
+        ],
+        name="rows_" + kind,
+    )(*inputs.values())
+
+
+def col_kernel(spec, x_ref, p_ref, w_ref, t_ref, y_ref, hi, lo, zs):
+    rows, quarter, devs = spec.rows, spec.quarter, spec.devs
+    count_in, count_out, sign = spec.count_in, spec.count_out, spec.sign
+    count = p_ref.shape[1]
+    per = devs // 4
+    weights = (w_ref[0], w_ref[1])
+
+    def spread(i, carry):
+        here = pl.ds(pl.multiple_of(i * rows, rows), rows)
+        for l in range(count_in):
+            x0, x1, x2, x3 = [x_ref[per * a + i, l] for a in range(4)]
+            s, t, d, e = x0 + x2, x1 + x3, x0 - x2, turn(x1 - x3)
+            for j, value in enumerate((s + t, d + e, s - t, d - e)):
+                if j:
+                    value = value * t_ref[0, j - 1, here, :] + turn(value) * t_ref[1, j - 1, here, :]
+                high, low = split(value)
+                hi[j, here, l * lanes : (l + 1) * lanes] = high
+                lo[j, here, l * lanes : (l + 1) * lanes] = low
+        return carry
+
+    lax.fori_loop(0, per, spread, 0)
+    wide_in, wide_out = count_in * lanes, count_out * lanes
+    for j in range(4):
+        y = dot3(weights, (hi[j, :, :wide_in], lo[j, :, :wide_in]))
+        spectra = []
+        for l in range(count_in):
+            at = slice(l * lanes, (l + 1) * lanes)
+            spectra.append(y[:quarter, at] + turn(y[quarter:, at]))
+        results = []
+        for l in range(count):
+            z = spectra[l if count_in > 1 else 0]
+            results.append(z * p_ref[0, l, j] - sign * (turn(z) * p_ref[1, l, j]))
+        if count_out == 1:
+            results = [sum(results)]
+        for l in range(count_out):
+            high, low = split(results[l])
+            hi[j, :, l * lanes : (l + 1) * lanes] = high
+            lo[j, :, l * lanes : (l + 1) * lanes] = low
+    for j in range(4):
+        y = dot3(weights, (hi[j, :, :wide_out], lo[j, :, :wide_out]))
+        for l in range(count_out):
+            at = slice(l * lanes, (l + 1) * lanes)
+            value = y[:quarter, at] - turn(y[quarter:, at])
+            if j:
+                value = value * t_ref[0, j - 1] - turn(value) * t_ref[1, j - 1]
+            zs[j, :, at] = value
+
+    def gather(i, carry):
+        here = pl.ds(pl.multiple_of(i * rows, rows), rows)
+        for l in range(count_out):
+            at = slice(l * lanes, (l + 1) * lanes)
+            g0, g1, g2, g3 = [zs[j, here, at] for j in range(4)]
+            s, t, d, e = g0 + g2, g1 + g3, g0 - g2, turn(g1 - g3)
+            for a, value in enumerate((s + t, d - e, s - t, d + e)):
+                y_ref[per * a + i, l] = value
+        return carry
+
+    lax.fori_loop(0, per, gather, 0)
+
+
+def run_cols(x, prop, tables, dims, count_in, count_out, sign):
+    spec = Names(**vars(dims), count_in=count_in, count_out=count_out, sign=sign)
+    rows, quarter, devs = dims.rows, dims.quarter, dims.devs
+    wide = max(count_in, count_out) * lanes
+    vmem = pl.BlockSpec(memory_space=pltpu.VMEM)
+    return pl.pallas_call(
+        functools.partial(col_kernel, spec),
+        out_shape=jax.ShapeDtypeStruct((devs, count_out, rows, lanes), f32),
+        in_specs=[vmem] * 4,
+        out_specs=vmem,
+        scratch_shapes=[
+            pltpu.VMEM((4, quarter, wide), bf16),
+            pltpu.VMEM((4, quarter, wide), bf16),
+            pltpu.VMEM((4, quarter, wide), f32),
+        ],
+        name="cols",
+    )(x, prop, jnp.asarray(tables.both), jnp.asarray(tables.twiddle))
+
+
+def band_kernel(spec, x_ref, p_ref, w_ref, v_ref, y_ref):
+    devs, sign, count = spec.devs, spec.sign, spec.count
+    half = lanes // 2
+    lane = lax.broadcasted_iota(jnp.int32, x_ref.shape[1:], 1)
+    pieces = [[], []]
+    for s in range(0, devs, 2):
+        even, odd = x_ref[s], x_ref[s + 1]
+        pieces[0].append(jnp.where(lane < half, even, pltpu.roll(odd, half, 1)))
+        pieces[1].append(jnp.where(lane < half, pltpu.roll(even, half, 1), odd))
+    field = jnp.concatenate([jnp.concatenate(p, 1) for p in pieces], 0)
+    wide = w_ref.shape[2] // 2
+    deep = v_ref.shape[2] // 2
+    cols = x_ref.shape[1] // 2
+    both = dot3(split(field), (w_ref[0], w_ref[1]))
+    scaled = []
+    for l in range(count):
+        re = slice(2 * l * cols, (2 * l + 1) * cols)
+        im = slice((2 * l + 1) * cols, (2 * l + 2) * cols)
+        yr = both[re, :wide] + both[im, wide:]
+        yi = both[im, :wide] - both[re, wide:]
+        pr, pi = p_ref[0], sign * p_ref[1]
+        scaled += [yr * pr - yi * pi, yr * pi + yi * pr]
+    both = dot3(split(jnp.concatenate(scaled, 0)), (v_ref[0], v_ref[1]))
+    out = []
+    for l in range(count):
+        re = slice(2 * l * cols, (2 * l + 1) * cols)
+        im = slice((2 * l + 1) * cols, (2 * l + 2) * cols)
+        out.append(
+            jnp.concatenate(
+                [both[re, :deep] - both[im, deep:], both[im, :deep] + both[re, deep:]], 0
+            )
+        )
+    for s in range(0, devs, 2):
+        at = slice(s * half, s * half + lanes)
+        first, second = out[0][:, at], out[1][:, at]
+        y_ref[s] = jnp.where(lane < half, first, pltpu.roll(second, half, 1))
+        y_ref[s + 1] = jnp.where(lane < half, pltpu.roll(first, half, 1), second)
+
+
+def run_band(x, pupil, tables, dims, sign):
+    vmem = pl.BlockSpec(memory_space=pltpu.VMEM)
+    return pl.pallas_call(
+        functools.partial(band_kernel, Names(**vars(dims), sign=sign)),
+        out_shape=jax.ShapeDtypeStruct(x.shape, f32),
+        in_specs=[vmem] * 4,
+        out_specs=vmem,
+        name="pupil_cols",
+    )(x, pupil, jnp.asarray(tables.band), jnp.asarray(tables.band_inv))
+
+
+def exchange(x):
+    return lax.all_to_all(x, "pat", split_axis=0, concat_axis=0, tiled=True)
+
+
+def body(slab_phase, pupil_phase, pupil_mask, led_code, led_freq, measured):
+    devs = lax.axis_size("pat")
+    position = lax.axis_index("pat")
+    slab_count, rows, size = slab_phase.shape
+    patterns, count = led_code.shape
+    quarter, cols, per = size // 4, size // devs, devs // 4
+    band = 2 * pupil_radius
+    band_cols = band // devs
+    dims = Names(
+        count=count, rows=rows, quarter=quarter, devs=devs, patterns=patterns,
+        area=float(size * size),
+    )
+    rt = row_tables(size, cols, band_cols)
+    ct = col_tables(size)
+    shape_full = (devs, count, rows, lanes)
+    shape_band = (devs, 2 * band_cols, count * rows)
+    shape_field = (2, count * rows, size)
+    transmission = [jnp.stack([jnp.cos(slab_phase[s]), jnp.sin(slab_phase[s])]) for s in range(slab_count)]
+    twiddle, table = rt.twiddle, rt
+
+    lane = jnp.arange(lanes, dtype=jnp.int32) % cols
+    col_index = 4 * ((position % per) * cols + lane) + position // per
+    row_index = 4 * jnp.arange(quarter, dtype=jnp.int32)[None, :] + jnp.arange(4, dtype=jnp.int32)[:, None]
+    col_freq = frequency(col_index[None, :] + led_freq[:, 1][:, None] + size, size)
+    row_freq = frequency(row_index[None] + led_freq[:, 0][:, None, None] + size, size)
+    radius = (row_freq * row_freq)[..., None] + (col_freq * col_freq)[:, None, None, :]
+    cutoff = size // 2 * (size // 2)
+    inside = radius <= cutoff
+    height = jnp.sqrt(jnp.maximum(cutoff - radius, 0).astype(f32))
+    shift = spread_rate * (height - size // 2)
+    prop = jnp.stack([jnp.where(inside, jnp.cos(shift), 0.0), jnp.where(inside, jnp.sin(shift), 0.0)])
+
+    def near(x):
+        return jnp.concatenate([x[:, size - pupil_radius :], x[:, :pupil_radius]], 1)
+
+    opening, phase = near(pupil_mask).astype(f32), near(pupil_phase)
+    own = jnp.stack([opening * jnp.cos(phase), opening * jnp.sin(phase)])
+    own = own.reshape(2, cols // 4, 4, band)
+    pupil = 0.0
+    owners = [(q - pupil_radius // cols) % devs for q in range(per)]
+    for j in range(4):
+        pairs = [(owners[q], per * j + q) for q in range(per)]
+        pupil = pupil + lax.ppermute(own[:, :, j], "pat", pairs)
+
+    def wave(freq, index):
+        turns = (freq[:, None] * index[None, :]) % size
+        angle = turns.astype(f32) * (2.0 * math.pi / size)
+        return jnp.stack([jnp.cos(angle), jnp.sin(angle)], 1).reshape(2 * count, -1)
+
+    tilt_c = wave(led_freq[:, 1], jnp.arange(size, dtype=jnp.int32))
+    tilt_r = wave(led_freq[:, 0], position * rows + jnp.arange(rows, dtype=jnp.int32))
+    tilt_r = jnp.broadcast_to(tilt_r[:, :, None], (2 * count, rows, lanes))
+    tilts = dict(tilt_r=tilt_r, tilt_c=tilt_c)
+    full_both = dict(inv=table.full_inv, fwd=table.full, twiddle=twiddle)
+
+    one = Names(**{**vars(dims), **dict(count=1)})
+    (y,) = run_rows(
+        "enter", None, "full", one,
+        dict(tr=transmission[0], fwd=table.full, twiddle=twiddle),
+        dict(y=(devs, 1, rows, lanes)),
+    )
+    x = exchange(run_cols(exchange(y), prop, ct, dims, 1, count, 1.0))
+    y, passed1 = run_rows(
+        "forward", "full", "full", dims, dict(x=x, tr=transmission[1], **full_both),
+        dict(y=shape_full, passed=shape_field),
+    )
+    x = exchange(run_cols(exchange(y), prop, ct, dims, count, count, 1.0))
+    y, passed2 = run_rows(
+        "forward_band", "full", "band", dims,
+        dict(x=x, tr=transmission[2], inv=table.full_inv, fwd=table.band, twiddle=twiddle, **tilts),
+        dict(y=shape_band, passed=shape_field),
+    )
+    x = exchange(run_band(exchange(y), pupil, ct, dims, 1.0))
+    stat_rows = count + count * (count + 1) // 2 + patterns * count + patterns
+    dims.stat_rows = stat_rows
+    camera, sums = run_rows(
+        "stats", "band", None, dims,
+        dict(x=x, inv=table.band_inv, twiddle=twiddle, measured=measured),
+        dict(passed=shape_field, sums=(devs, -(-stat_rows // 8) * 8, lanes)),
+    )
+    (y,) = run_rows(
+        "weigh", None, "band", dims,
+        dict(stats=exchange(sums), code=led_code, passed=camera, measured=measured, fwd=table.band, twiddle=twiddle),
+        dict(y=shape_band),
+    )
+    x = exchange(run_band(exchange(y), pupil, ct, dims, -1.0))
+    y, grad2 = run_rows(
+        "back_band", "band", "full", dims,
+        dict(x=x, tr=transmission[2], passed=passed2, inv=table.band_inv, fwd=table.full, twiddle=twiddle, **tilts),
+        dict(y=shape_full, grad=(rows, size)),
+    )
+    x = exchange(run_cols(exchange(y), prop, ct, dims, count, count, -1.0))
+    y, grad1 = run_rows(
+        "back", "full", "full", dims,
+        dict(x=x, tr=transmission[1], passed=passed1, **full_both),
+        dict(y=shape_full, grad=(rows, size)),
+    )
+    x = exchange(run_cols(exchange(y), prop, ct, dims, count, 1, -1.0))
+    (grad0,) = run_rows(
+        "leave", "full", None, one,
+        dict(x=x, tr=transmission[0], inv=table.full_inv, twiddle=twiddle),
+        dict(grad=(rows, size)),
+    )
+    return jnp.stack([grad0, grad1, grad2])
+
+
 def solution(mesh):
     in_specs = (
         P("tiles", "pat", None),
@@ -190,4 +752,13 @@
         P("tiles", "pat", None),
     )
     out_specs = P("tiles", "pat", None)
-    return jax.shard_map(body, mesh=mesh, in_specs=in_specs, out_specs=out_specs, check_vma=False)
+    def run(slab_phase, *others):
+        devs = mesh.shape["pat"]
+        size, count = slab_phase.shape[-1], others[2].shape[1]
+        fits = 2 * size == lanes * devs and count * size == lanes * devs and slab_phase.shape[0] == 3 * mesh.shape["tiles"]
+        inner = body if fits else plain_body
+        return jax.shard_map(inner, mesh=mesh, in_specs=in_specs, out_specs=out_specs, check_vma=False)(
+            slab_phase, *others
+        )
+
+    return run

time: 798 us -> 382 us (0.48); the launches traced: 786 us -> 380 us
  local copies, waits for them, and re-layouts: 164 us -> 11.3 us
  waiting for transfers between devices: 202 us -> 59.2 us
  matrix products: 142 us -> 0 us
  Pallas kernels: 0 us -> 72.4 us
  other arithmetic: 83.2 us -> 11.7 us
  blocking collectives: 127 us -> 184 us
  starting transfers between devices: 65 us -> 41.4 us
    all_to_all x10 -> x5, waiting for transfers between devices: 202 us -> 57.7 us  [exchange(): return lax.all_to_all(x, 'pat', split_axis=0, concat_axis=0, tiled=True)]
    dot_general x50 -> x0, matrix products: 142 us -> none  [the longest x6 26 us: to_fourier(): jnp.einsum('swlcr,wsvj->vlcrj', incoming, long_table, precision=highest)]
    all_to_all x2 -> x8, blocking collectives: 62.5 us -> 184 us  [exchange(): return lax.all_to_all(x, 'pat', split_axis=0, concat_axis=0, tiled=True)]
    pallas_call x0 -> x14, Pallas kernels: none -> 72.4 us  [the longest x8 36.6 us: run_rows(): pl.pallas_call(functools.partial(row_kernel, spec), out_shape=[jax.ShapeD...]
    psum x2 -> x0, blocking collectives: 64.8 us -> none  [the longest x1 34.9 us: body(): lax.psum((jnp.sum(pattern_power, axis=(1, 2)), jnp.sum(counts, axis=(1, 2...]
    all_to_all x12 -> x0, other arithmetic: 40.2 us -> none  [the longest x6 21.4 us: to_fourier(): lax.all_to_all(outgoing.reshape(dev_count, -1), 'pat', split_axis=0, conc...]
    another operation x14 -> x0, local copies, waits for them, and re-layouts: 39.9 us -> none  [the longest x12 33.1 us: complex_times(): return jnp.stack([real_part, imag_part])]
    all_to_all x10 -> x5, starting transfers between devices: 65 us -> 26.9 us  [exchange(): return lax.all_to_all(x, 'pat', split_axis=0, concat_axis=0, tiled=True)]
  transfers between devices with their start and end apart: 10 -> 9, of which waited for: 10 -> 6; matrix products, arithmetic and copies ran while one was open for 3% -> 3% of each run, Pallas kernels for 0% -> 0%
where the time goes in v1:
time: 382 us; the launch traced here: 380 us
  blocking collectives  184 us (48%)
  Pallas kernels  72.4 us (19%)
  waiting for transfers between devices  59.2 us (15%)
  starting transfers between devices  41.4 us (11%)
  other arithmetic  11.7 us (3%)
  local copies, waits for them, and re-layouts  11.3 us (3%)
    all_to_all x8, blocking collectives, exchange(): return lax.all_to_all(x, 'pat', split_axis=0, concat_axis=0, tiled=True)  184 us
    all_to_all x5, waiting for transfers between devices, exchange(): return lax.all_to_all(x, 'pat', split_axis=0, concat_axis=0, tiled=True)  57.7 us
    pallas_call x8, Pallas kernels, run_rows(): pl.pallas_call(functools.partial(row_kernel, spec), out_shape=[jax.ShapeD...  36.6 us
    all_to_all x5, starting transfers between devices, exchange(): return lax.all_to_all(x, 'pat', split_axis=0, concat_axis=0, tiled=True)  26.9 us
    pallas_call x4, Pallas kernels, run_cols(): pl.pallas_call(functools.partial(col_kernel, spec), out_shape=jax.ShapeDt...  25.5 us
    ppermute x4, starting transfers between devices, body(): pupil = pupil + lax.ppermute(own[:, :, j], 'pat', pairs)  14.6 us
    pallas_call x2, Pallas kernels, run_band(): pl.pallas_call(functools.partial(band_kernel, Names(**vars(dims), sign=si...  10.3 us
  transfers between devices with their start and end apart: 9, of which 6 were waited for; matrix products, arithmetic and copies ran while one was open for 3% of the time, Pallas kernels for 0%

profile of v1, /device:TPU:0, one launch (start us, length us, event | category | flops | bytes accessed | tf_op | source)
XLA Modules:
  0.0 380.1 jit_solution(9731722252954439026)
XLA Ops:
  8.3 7.4 %all-to-all-start = ((f32[16,1,64,128]{3,2,1,0:T(8,128)}), f32[16,1,64,128]{3,2,1,0:T(8,128)S(1)}, u32[]{:S(2)}, u32[]{:S(2)}) async-start(f32[16,1,64,128]{3,2,1,0:T(8,128)} %rows_enter.1), calls=%async_computation | async-start | bytes 1048576 | tf_op jit(solution)/shard_map/all_to_all | solution.py:636
  21.8 8.1 %all-to-all-done.x_ref = f32[16,1,64,128]{3,2,1,0:T(8,128)S(1)} async-done(((f32[16,1,64,128]{3,2,1,0:T(8,128)}), f32[16,1,64,128]{3,2,1,0:T(8,128)S(1)}, u32[]{:S(2)}, u32[]{:S(2)}) %all-to-all-start) | async-done | bytes 524320 | tf_op jit(solution)/shard_map/all_to_all | solution.py:636
  30.8 6.3 %cols.4 = f32[16,2,64,128]{3,2,1,0:T(8,128)} custom-call(f32[16,1,64,128]{3,2,1,0:T(8,128)} %copy-done.2, f32[2,2,4,256,128]{4,3,2,1,0:T(8,128)} %pad_maximum_fusion.p_ref, bf16[2,512,256]{2,1,0:T(8,128)(2,1)} %constant.131.clone.w_ref, f32[2,3,256,128]{3,2,1,0:T(8,128)} %constant.132.clone.t_ref), custom_call_target="tpu_custom_call" | custom-call | tf_op jit(solution)/shard_map/cols/pallas_call | solution.py:571
  42.1 22.0 %all-to-all-done.1.refs_0_ = f32[16,2,64,128]{3,2,1,0:T(8,128)S(1)} async-done(((f32[16,2,64,128]{3,2,1,0:T(8,128)}), f32[16,2,64,128]{3,2,1,0:T(8,128)S(1)}, u32[]{:S(2)}, u32[]{:S(2)}) %all-to-all-start.1) | async-done | bytes 1048608 | tf_op jit(solution)/shard_map/all_to_all | solution.py:636
  65.1 5.5 %rows_forward.1 = (f32[16,2,64,128]{3,2,1,0:T(8,128)}, f32[2,128,1024]{2,1,0:T(8,128)}) custom-call(f32[16,2,64,128]{3,2,1,0:T(8,128)} %copy-done.1, f32[2,64,1024]{2,1,0:T(8,128)} %pad_maximum_fusion.3.refs_1_, bf16[2,512,512]{2,1,0:T(8,128)(2,1)} %constant.127.clone.refs_2_.refs_3_, bf16[2,512,512]{2,1,0:T(8,128)(2,1)} %constant.126.clone.refs_1_.refs_3_.refs_4_, ...), custom_call_target="tpu_custom_call" | custom-call | tf_op jit(solution)/shard_map/rows_forward/pallas_call | solution.py:492
  70.7 31.6 %all_to_all.65.x_ref = f32[16,2,64,128]{3,2,1,0:T(8,128)} all-to-all(f32[16,2,64,128]{3,2,1,0:T(8,128)} %get-tuple-element.15), channel_id=1, replica_groups=mesh['tiles'=2,'pat'=16] {'pat'}, dimensions={0} | all-to-all | bytes 2097152 | tf_op jit(solution)/shard_map/all_to_all | solution.py:636
  102.2 6.5 %cols.5 = f32[16,2,64,128]{3,2,1,0:T(8,128)} custom-call(f32[16,2,64,128]{3,2,1,0:T(8,128)} %all_to_all.65.x_ref, f32[2,2,4,256,128]{4,3,2,1,0:T(8,128)} %pad_maximum_fusion.p_ref, bf16[2,512,256]{2,1,0:T(8,128)(2,1)} %constant.131.clone.w_ref, f32[2,3,256,128]{3,2,1,0:T(8,128)} %constant.132.clone.t_ref), custom_call_target="tpu_custom_call" | custom-call | tf_op jit(solution)/shard_map/cols/pallas_call | solution.py:571
  117.4 19.3 %all-to-all-done.3.refs_0_ = f32[16,2,64,128]{3,2,1,0:T(8,128)S(1)} async-done(((f32[16,2,64,128]{3,2,1,0:T(8,128)}), f32[16,2,64,128]{3,2,1,0:T(8,128)S(1)}, u32[]{:S(2)}, u32[]{:S(2)}) %all-to-all-start.3) | async-done | bytes 1048608 | tf_op jit(solution)/shard_map/all_to_all | solution.py:636
  142.7 6.8 %all-to-all-start.4 = ((f32[16,32,128]{2,1,0:T(8,128)}), f32[16,32,128]{2,1,0:T(8,128)S(1)}, u32[]{:S(2)}, u32[]{:S(2)}) async-start(f32[16,32,128]{2,1,0:T(8,128)} %get-tuple-element.16), calls=%async_computation.4 | async-start | bytes 524288 | tf_op jit(solution)/shard_map/all_to_all | solution.py:636
  156.4 6.6 %collective-permute-start.3 = (f32[2,16,256]{2,1,0:T(8,128)S(1)}, f32[2,16,256]{2,1,0:T(8,128)S(1)}, u32[]{:S(2)}, u32[]{:S(2)}) collective-permute-start(f32[2,16,256]{2,1,0:T(8,128)S(1)} %get-tuple-element.39), channel_id=1, source_target_pairs={{14,12},{15,13},{0,14},{1,15},{30,28},{31,29},{16,30},{17,31}} | collective-permute-start | bytes 98312 | tf_op jit(solution)/shard_map/ppermute | solution.py:681
  167.3 5.2 %pupil_cols.2 = f32[16,32,128]{2,1,0:T(8,128)} custom-call(f32[16,32,128]{2,1,0:T(8,128)} %copy-done.3, f32[2,16,256]{2,1,0:T(8,128)} %add_add_fusion.p_ref, bf16[2,1024,512]{2,1,0:T(8,128)(2,1)} %constant.133.clone.w_ref, bf16[2,256,2048]{2,1,0:T(8,128)(2,1)} %constant.134.clone.v_ref), custom_call_target="tpu_custom_call" | custom-call | tf_op jit(solution)/shard_map/pupil_cols/pallas_call | solution.py:626
  172.4 15.7 %all_to_all.66.refs_0_ = f32[16,32,128]{2,1,0:T(8,128)} all-to-all(f32[16,32,128]{2,1,0:T(8,128)} %pupil_cols.2), channel_id=1, replica_groups=mesh['tiles'=2,'pat'=16] {'pat'}, dimensions={0} | all-to-all | bytes 524288 | tf_op jit(solution)/shard_map/all_to_all | solution.py:636
  196.0 8.3 %all-to-all-done.6.refs_0_ = f32[16,24,128]{2,1,0:T(8,128)S(1)} async-done(((f32[16,24,128]{2,1,0:T(8,128)}), f32[16,24,128]{2,1,0:T(8,128)S(1)}, u32[]{:S(2)}, u32[]{:S(2)}) %all-to-all-start.6) | async-done | bytes 196640 | tf_op jit(solution)/shard_map/all_to_all | solution.py:636
  209.0 14.2 %all_to_all.67.x_ref = f32[16,32,128]{2,1,0:T(8,128)} all-to-all(f32[16,32,128]{2,1,0:T(8,128)} %rows_weigh.1), channel_id=1, replica_groups=mesh['tiles'=2,'pat'=16] {'pat'}, dimensions={0} | all-to-all | bytes 524288 | tf_op jit(solution)/shard_map/all_to_all | solution.py:636
  223.2 5.2 %pupil_cols.3 = f32[16,32,128]{2,1,0:T(8,128)} custom-call(f32[16,32,128]{2,1,0:T(8,128)} %all_to_all.67.x_ref, f32[2,16,256]{2,1,0:T(8,128)} %add_add_fusion.p_ref, bf16[2,1024,512]{2,1,0:T(8,128)(2,1)} %constant.133.clone.w_ref, bf16[2,256,2048]{2,1,0:T(8,128)(2,1)} %constant.134.clone.v_ref), custom_call_target="tpu_custom_call" | custom-call | tf_op jit(solution)/shard_map/pupil_cols/pallas_call | solution.py:626
  228.3 14.2 %all_to_all.68.refs_0_ = f32[16,32,128]{2,1,0:T(8,128)} all-to-all(f32[16,32,128]{2,1,0:T(8,128)} %pupil_cols.3), channel_id=1, replica_groups=mesh['tiles'=2,'pat'=16] {'pat'}, dimensions={0} | all-to-all | bytes 524288 | tf_op jit(solution)/shard_map/all_to_all | solution.py:636
  242.5 5.3 %rows_back_band.1 = (f32[16,2,64,128]{3,2,1,0:T(8,128)}, f32[64,1024]{1,0:T(8,128)}) custom-call(f32[16,32,128]{2,1,0:T(8,128)} %all_to_all.68.refs_0_, f32[2,64,1024]{2,1,0:T(8,128)} %pad_maximum_fusion.4.refs_1_, f32[2,128,1024]{2,1,0:T(8,128)} %get-tuple-element.19.refs_2_, bf16[2,128,512]{2,1,0:T(8,128)(2,1)} %constant.129.clone.refs_1_.refs_3_, ...), custom_call_target="tpu_custom_call" | custom-call | tf_op jit(solution)/shard_map/rows_back_band/pallas_call | solution.py:492
  247.9 29.0 %all_to_all.69.x_ref = f32[16,2,64,128]{3,2,1,0:T(8,128)} all-to-all(f32[16,2,64,128]{3,2,1,0:T(8,128)} %get-tuple-element.20), channel_id=1, replica_groups=mesh['tiles'=2,'pat'=16] {'pat'}, dimensions={0} | all-to-all | bytes 2097152 | tf_op jit(solution)/shard_map/all_to_all | solution.py:636
  276.9 6.6 %cols.6 = f32[16,2,64,128]{3,2,1,0:T(8,128)} custom-call(f32[16,2,64,128]{3,2,1,0:T(8,128)} %all_to_all.69.x_ref, f32[2,2,4,256,128]{4,3,2,1,0:T(8,128)} %pad_maximum_fusion.p_ref, bf16[2,512,256]{2,1,0:T(8,128)(2,1)} %constant.131.clone.w_ref, f32[2,3,256,128]{3,2,1,0:T(8,128)} %constant.132.clone.t_ref), custom_call_target="tpu_custom_call" | custom-call | tf_op jit(solution)/shard_map/cols/pallas_call | solution.py:571
  283.4 29.7 %all_to_all.70.refs_0_ = f32[16,2,64,128]{3,2,1,0:T(8,128)} all-to-all(f32[16,2,64,128]{3,2,1,0:T(8,128)} %cols.6), channel_id=1, replica_groups=mesh['tiles'=2,'pat'=16] {'pat'}, dimensions={0} | all-to-all | bytes 2097152 | tf_op jit(solution)/shard_map/all_to_all | solution.py:636
  313.1 6.0 %rows_back.1 = (f32[16,2,64,128]{3,2,1,0:T(8,128)}, f32[64,1024]{1,0:T(8,128)}) custom-call(f32[16,2,64,128]{3,2,1,0:T(8,128)} %all_to_all.70.refs_0_, f32[2,64,1024]{2,1,0:T(8,128)} %pad_maximum_fusion.3.refs_1_, f32[2,128,1024]{2,1,0:T(8,128)} %get-tuple-element.21.refs_2_, bf16[2,512,512]{2,1,0:T(8,128)(2,1)} %constant.127.clone.refs_2_.refs_3_, ...), custom_call_target="tpu_custom_call" | custom-call | tf_op jit(solution)/shard_map/rows_back/pallas_call | solution.py:492
  319.1 29.8 %all_to_all.71.x_ref = f32[16,2,64,128]{3,2,1,0:T(8,128)} all-to-all(f32[16,2,64,128]{3,2,1,0:T(8,128)} %get-tuple-element.22), channel_id=1, replica_groups=mesh['tiles'=2,'pat'=16] {'pat'}, dimensions={0} | all-to-all | bytes 2097152 | tf_op jit(solution)/shard_map/all_to_all | solution.py:636
  348.9 6.2 %cols.7 = f32[16,1,64,128]{3,2,1,0:T(8,128)} custom-call(f32[16,2,64,128]{3,2,1,0:T(8,128)} %all_to_all.71.x_ref, f32[2,2,4,256,128]{4,3,2,1,0:T(8,128)} %pad_maximum_fusion.p_ref, bf16[2,512,256]{2,1,0:T(8,128)(2,1)} %constant.131.clone.w_ref, f32[2,3,256,128]{3,2,1,0:T(8,128)} %constant.132.clone.t_ref), custom_call_target="tpu_custom_call" | custom-call | tf_op jit(solution)/shard_map/cols/pallas_call | solution.py:571
  355.1 19.5 %all_to_all.72.refs_0_ = f32[16,1,64,128]{3,2,1,0:T(8,128)} all-to-all(f32[16,1,64,128]{3,2,1,0:T(8,128)} %cols.7), channel_id=1, replica_groups=mesh['tiles'=2,'pat'=16] {'pat'}, dimensions={0} | all-to-all | bytes 1048576 | tf_op jit(solution)/shard_map/all_to_all | solution.py:636
  (64 shorter events, 64.9 us)
Async XLA Ops:
  3.9 11.8 %copy-start.7 = (s32[2,2]{1,0:T(2,128)S(1)}, s32[2,2]{1,0:T(2,128)}, u32[]{:S(2)}) copy-start(s32[2,2]{1,0:T(2,128)} %param.19) | copy-start | bytes 52
  8.3 21.7 %all-to-all-start = ((f32[16,1,64,128]{3,2,1,0:T(8,128)}), f32[16,1,64,128]{3,2,1,0:T(8,128)S(1)}, u32[]{:S(2)}, u32[]{:S(2)}) async-start(f32[16,1,64,128]{3,2,1,0:T(8,128)} %rows_enter.1), calls=%async_computation | async-start | bytes 1048576 | tf_op jit(solution)/shard_map/all_to_all | solution.py:636
  29.9 0.8 copy-start.2
  37.0 27.1 %all-to-all-start.1 = ((f32[16,2,64,128]{3,2,1,0:T(8,128)}), f32[16,2,64,128]{3,2,1,0:T(8,128)S(1)}, u32[]{:S(2)}, u32[]{:S(2)}) async-start(f32[16,2,64,128]{3,2,1,0:T(8,128)} %cols.4), calls=%async_computation.1 | async-start | bytes 2097152 | tf_op jit(solution)/shard_map/all_to_all | solution.py:636
  64.1 1.0 copy-start.1
  108.7 27.9 %all-to-all-start.3 = ((f32[16,2,64,128]{3,2,1,0:T(8,128)}), f32[16,2,64,128]{3,2,1,0:T(8,128)S(1)}, u32[]{:S(2)}, u32[]{:S(2)}) async-start(f32[16,2,64,128]{3,2,1,0:T(8,128)} %cols.5), calls=%async_computation.3 | async-start | bytes 2097152 | tf_op jit(solution)/shard_map/all_to_all | solution.py:636
  136.7 1.1 copy-start
  142.7 23.9 %all-to-all-start.4 = ((f32[16,32,128]{2,1,0:T(8,128)}), f32[16,32,128]{2,1,0:T(8,128)S(1)}, u32[]{:S(2)}, u32[]{:S(2)}) async-start(f32[16,32,128]{2,1,0:T(8,128)} %get-tuple-element.16), calls=%async_computation.4 | async-start | bytes 524288 | tf_op jit(solution)/shard_map/all_to_all | solution.py:636
  149.8 14.6 %collective-permute-start.1 = (f32[2,16,256]{2,1,0:T(8,128)S(1)}, f32[2,16,256]{2,1,0:T(8,128)S(1)}, u32[]{:S(2)}, u32[]{:S(2)}) collective-permute-start(f32[2,16,256]{2,1,0:T(8,128)S(1)} %get-tuple-element.37), channel_id=1, source_target_pairs={{14,4},{15,5},{0,6},{1,7},{30,20},{31,21},{16,22},{17,23}} | collective-permute-start | bytes 98312 | tf_op jit(solution)/shard_map/ppermute | solution.py:681
  154.5 9.9 %collective-permute-start = (f32[2,16,256]{2,1,0:T(8,128)S(1)}, f32[2,16,256]{2,1,0:T(8,128)S(1)}, u32[]{:S(2)}, u32[]{:S(2)}) collective-permute-start(f32[2,16,256]{2,1,0:T(8,128)S(1)} %get-tuple-element.38), channel_id=1, source_target_pairs={{14,0},{15,1},{0,2},{1,3},{30,16},{31,17},{16,18},{17,19}} | collective-permute-start | bytes 98312 | tf_op jit(solution)/shard_map/ppermute | solution.py:681
  156.4 8.3 %collective-permute-start.3 = (f32[2,16,256]{2,1,0:T(8,128)S(1)}, f32[2,16,256]{2,1,0:T(8,128)S(1)}, u32[]{:S(2)}, u32[]{:S(2)}) collective-permute-start(f32[2,16,256]{2,1,0:T(8,128)S(1)} %get-tuple-element.39), channel_id=1, source_target_pairs={{14,12},{15,13},{0,14},{1,15},{30,28},{31,29},{16,30},{17,31}} | collective-permute-start | bytes 98312 | tf_op jit(solution)/shard_map/ppermute | solution.py:681
  163.0 2.9 collective-permute-start.2
  166.5 0.7 copy-start.3
  172.4 22.9 %copy-start.8 = (s32[4,2]{0,1:T(2,128)S(1)}, s32[4,2]{0,1:T(2,128)}, u32[]{:S(2)}) copy-start(s32[4,2]{0,1:T(2,128)} %param.18) | copy-start | bytes 100
  191.8 12.5 %all-to-all-start.6 = ((f32[16,24,128]{2,1,0:T(8,128)}), f32[16,24,128]{2,1,0:T(8,128)S(1)}, u32[]{:S(2)}, u32[]{:S(2)}) async-start(f32[16,24,128]{2,1,0:T(8,128)} %get-tuple-element.17), calls=%async_computation.6 | async-start | bytes 393216 | tf_op jit(solution)/shard_map/all_to_all | solution.py:636
  204.3 0.7 copy-start.4
  355.1 23.1 %copy-start.5 = (f32[64,1024]{1,0:T(8,128)S(1)}, f32[64,1024]{1,0:T(8,128)}, u32[]{:S(2)}) copy-start(f32[64,1024]{1,0:T(8,128)} %get-tuple-element.24) | copy-start | bytes 786436
  355.1 23.1 %copy-start.6 = (f32[64,1024]{1,0:T(8,128)S(1)}, f32[64,1024]{1,0:T(8,128)}, u32[]{:S(2)}) copy-start(f32[64,1024]{1,0:T(8,128)} %get-tuple-element.23) | copy-start | bytes 786436

commit v2 on v1

--- a/solution.py
+++ b/solution.py
@@ -267,6 +267,79 @@
     return jnp.where(lane < lanes // 2, rolled, -rolled)
 
 
+def partner(me, step, devs):
+    return lax.rem(me + step, devs)
+
+
+def greet(devs):
+    me = lax.axis_index("pat")
+    barrier = pltpu.get_barrier_semaphore()
+
+    def signal(step, carry):
+        pl.semaphore_signal(
+            barrier, inc=1, device_id=dict(pat=partner(me, step, devs)),
+            device_id_type=pl.DeviceIdType.MESH,
+        )
+        return carry
+
+    lax.fori_loop(1, devs, signal, 0)
+    return me, barrier
+
+
+def remote(ref, me, dest):
+    block = ref.stage if ref.same else ref.stage.at[dest]
+    return pltpu.make_async_remote_copy(
+        src_ref=block, dst_ref=ref.y.at[me], send_sem=ref.sent.at[dest],
+        recv_sem=ref.got.at[me], device_id=dict(pat=dest), device_id_type=pl.DeviceIdType.MESH,
+    )
+
+
+def send(ref, me, dest):
+    @pl.when(dest != me)
+    def _():
+        remote(ref, me, dest).start()
+
+    @pl.when(dest == me)
+    def _():
+        keep(ref, me).start()
+
+
+def keep(ref, me):
+    block = ref.stage if ref.same else ref.stage.at[me]
+    return pltpu.make_async_copy(block, ref.y.at[me], ref.kept)
+
+
+def finish(ref, me, devs):
+    def settle(step, carry):
+        other = partner(me, step, devs)
+        block = ref.stage if ref.same else ref.stage.at[other]
+        pltpu.make_async_remote_copy(
+            src_ref=block, dst_ref=ref.y.at[other], send_sem=ref.sent.at[other],
+            recv_sem=ref.got.at[other], device_id=dict(pat=other),
+            device_id_type=pl.DeviceIdType.MESH,
+        ).wait()
+        return carry
+
+    keep(ref, me).wait()
+    lax.fori_loop(1, devs, settle, 0)
+
+
+def comm_scratch(stage_shape, devs):
+    return [
+        pltpu.VMEM(stage_shape, f32),
+        pltpu.SemaphoreType.DMA((devs,)),
+        pltpu.SemaphoreType.DMA((devs,)),
+        pltpu.SemaphoreType.DMA,
+    ]
+
+
+def comm_params(channel):
+    return pltpu.CompilerParams(collective_id=channel, has_side_effects=True)
+
+
+anywhere = pl.BlockSpec(memory_space=pl.ANY)
+
+
 def row_spread(blocks, twiddle_ref):
     (r0, i0), (r1, i1), (r2, i2), (r3, i3) = blocks
     sr, si, tr, ti = r0 + r2, i0 + i2, r1 + r3, i1 + i3
@@ -293,7 +366,10 @@
 
 
 def row_kernel(spec, *refs):
-    ref = Names(**dict(zip(spec.names, refs)))
+    ref = Names(**dict(zip(spec.names, refs)), same=spec.kind == "stats")
+    sends = spec.kind != "leave"
+    if sends:
+        me, barrier = greet(spec.devs)
     count, rows, quarter = spec.count, spec.rows, spec.quarter
     devs = spec.devs
     per = devs // 4
@@ -461,29 +537,54 @@
     if kind == "stats":
         stats = lax.fori_loop(0, rows // step, chunk, tuple(stats))
         packed = [jnp.sum(row, 0, keepdims=True) for row in stats]
-        packed.append(jnp.zeros((ref.sums.shape[1] - len(packed), lanes), f32))
+        packed.append(jnp.zeros((ref.stage.shape[0] - len(packed), lanes), f32))
         packed = jnp.concatenate(packed, 0)
-        for d in range(devs):
-            ref.sums[d] = packed
+        ref.stage[...] = packed
+        pl.semaphore_wait(barrier, devs - 1)
+
+        def share(k, carry):
+            send(ref, me, partner(me, k, devs))
+            return carry
+
+        lax.fori_loop(0, devs, share, 0)
+        finish(ref, me, devs)
         return
     lax.fori_loop(0, rows // step, chunk, 0)
-    if spec.target == "full":
-        for j in range(4):
-            y = dot3((hi[j, :total, :], lo[j, :total, :]), (ref.fwd[0], ref.fwd[1]))
+    if not sends:
+        return
+    pl.semaphore_wait(barrier, devs - 1)
+
+    def emit(step_j, carry):
+        j = lax.rem(me // per + step_j, 4)
+        y = dot3((hi[j, :total, :], lo[j, :total, :]), (ref.fwd[0], ref.fwd[1]))
+        if spec.target == "full":
             for q in range(per):
-                ref.y[per * j + q] = y[:, q * lanes : (q + 1) * lanes].reshape(count, rows, lanes)
-    elif spec.target == "band":
-        for j in range(4):
-            y = dot3((hi[j, :total, :], lo[j, :total, :]), (ref.fwd[0], ref.fwd[1]))
-            ref.y[per * j : per * (j + 1)] = y.T.reshape(per, -1, total)
-
-
-def run_rows(kind, source, target, dims, inputs, outputs):
+                ref.stage[per * j + q] = y[:, q * lanes : (q + 1) * lanes].reshape(count, rows, lanes)
+        else:
+            flipped = y.T
+            deep = flipped.shape[0] // per
+            for q in range(per):
+                ref.stage[per * j + q] = flipped[q * deep : (q + 1) * deep]
+        for q in range(per):
+            send(ref, me, per * j + lax.rem(me + q, per))
+        return carry
+
+    lax.fori_loop(0, 4, emit, 0)
+    finish(ref, me, devs)
+
+
+def run_rows(channel, kind, source, target, dims, inputs, outputs):
     spec = Names(**vars(dims), kind=kind, source=source, target=target)
     count = spec.count
     total = count * spec.rows
     wide = 2 * spec.quarter
     names = list(inputs) + list(outputs) + ["hi", "lo", "zs"]
+    sends = "y" in outputs
+    comm = []
+    if sends:
+        names += ["stage", "sent", "got", "kept"]
+        shape = outputs["y"]
+        comm = comm_scratch(shape[1:] if kind == "stats" else shape, spec.devs)
     spec.names = names
     vmem = pl.BlockSpec(memory_space=pltpu.VMEM)
     in_specs = [
@@ -493,17 +594,21 @@
         functools.partial(row_kernel, spec),
         out_shape=[jax.ShapeDtypeStruct(shape, f32) for shape in outputs.values()],
         in_specs=in_specs,
-        out_specs=[vmem] * len(outputs),
+        out_specs=[anywhere if name == "y" else vmem for name in outputs],
         scratch_shapes=[
             pltpu.VMEM((4, total, wide), bf16),
             pltpu.VMEM((4, total, wide), bf16),
             pltpu.VMEM((4, total, wide), f32),
-        ],
+        ]
+        + comm,
+        compiler_params=comm_params(channel) if sends else None,
         name="rows_" + kind,
     )(*inputs.values())
 
 
-def col_kernel(spec, x_ref, p_ref, w_ref, t_ref, y_ref, hi, lo, zs):
+def col_kernel(spec, x_ref, p_ref, w_ref, t_ref, y_ref, hi, lo, zs, stage, sent, got, kept):
+    ref = Names(y=y_ref, stage=stage, sent=sent, got=got, kept=kept, same=False)
+    me, barrier = greet(spec.devs)
     rows, quarter, devs = spec.rows, spec.quarter, spec.devs
     count_in, count_out, sign = spec.count_in, spec.count_out, spec.sign
     count = p_ref.shape[1]
@@ -550,20 +655,26 @@
                 value = value * t_ref[0, j - 1] - turn(value) * t_ref[1, j - 1]
             zs[j, :, at] = value
 
-    def gather(i, carry):
+    pl.semaphore_wait(barrier, devs - 1)
+
+    def gather(step, carry):
+        i = lax.rem(me + step, per)
         here = pl.ds(pl.multiple_of(i * rows, rows), rows)
         for l in range(count_out):
             at = slice(l * lanes, (l + 1) * lanes)
             g0, g1, g2, g3 = [zs[j, here, at] for j in range(4)]
             s, t, d, e = g0 + g2, g1 + g3, g0 - g2, turn(g1 - g3)
             for a, value in enumerate((s + t, d - e, s - t, d + e)):
-                y_ref[per * a + i, l] = value
+                stage[per * a + i, l] = value
+        for a in range(4):
+            send(ref, me, lax.rem(me // per + a, 4) * per + i)
         return carry
 
     lax.fori_loop(0, per, gather, 0)
-
-
-def run_cols(x, prop, tables, dims, count_in, count_out, sign):
+    finish(ref, me, devs)
+
+
+def run_cols(channel, x, prop, tables, dims, count_in, count_out, sign):
     spec = Names(**vars(dims), count_in=count_in, count_out=count_out, sign=sign)
     rows, quarter, devs = dims.rows, dims.quarter, dims.devs
     wide = max(count_in, count_out) * lanes
@@ -572,17 +683,21 @@
         functools.partial(col_kernel, spec),
         out_shape=jax.ShapeDtypeStruct((devs, count_out, rows, lanes), f32),
         in_specs=[vmem] * 4,
-        out_specs=vmem,
+        out_specs=anywhere,
         scratch_shapes=[
             pltpu.VMEM((4, quarter, wide), bf16),
             pltpu.VMEM((4, quarter, wide), bf16),
             pltpu.VMEM((4, quarter, wide), f32),
-        ],
+        ]
+        + comm_scratch((devs, count_out, rows, lanes), devs),
+        compiler_params=comm_params(channel),
         name="cols",
     )(x, prop, jnp.asarray(tables.both), jnp.asarray(tables.twiddle))
 
 
-def band_kernel(spec, x_ref, p_ref, w_ref, v_ref, y_ref):
+def band_kernel(spec, x_ref, p_ref, w_ref, v_ref, y_ref, stage, sent, got, kept):
+    ref = Names(y=y_ref, stage=stage, sent=sent, got=got, kept=kept, same=False)
+    me, barrier = greet(spec.devs)
     devs, sign, count = spec.devs, spec.sign, spec.count
     half = lanes // 2
     lane = lax.broadcasted_iota(jnp.int32, x_ref.shape[1:], 1)
@@ -617,23 +732,29 @@
     for s in range(0, devs, 2):
         at = slice(s * half, s * half + lanes)
         first, second = out[0][:, at], out[1][:, at]
-        y_ref[s] = jnp.where(lane < half, first, pltpu.roll(second, half, 1))
-        y_ref[s + 1] = jnp.where(lane < half, pltpu.roll(first, half, 1), second)
-
-
-def run_band(x, pupil, tables, dims, sign):
+        stage[s] = jnp.where(lane < half, first, pltpu.roll(second, half, 1))
+        stage[s + 1] = jnp.where(lane < half, pltpu.roll(first, half, 1), second)
+    pl.semaphore_wait(barrier, devs - 1)
+
+    def share(k, carry):
+        send(ref, me, partner(me, k, devs))
+        return carry
+
+    lax.fori_loop(0, devs, share, 0)
+    finish(ref, me, devs)
+
+
+def run_band(channel, x, pupil, tables, dims, sign):
     vmem = pl.BlockSpec(memory_space=pltpu.VMEM)
     return pl.pallas_call(
         functools.partial(band_kernel, Names(**vars(dims), sign=sign)),
         out_shape=jax.ShapeDtypeStruct(x.shape, f32),
         in_specs=[vmem] * 4,
-        out_specs=vmem,
+        out_specs=anywhere,
+        scratch_shapes=comm_scratch(x.shape, dims.devs),
+        compiler_params=comm_params(channel),
         name="pupil_cols",
     )(x, pupil, jnp.asarray(tables.band), jnp.asarray(tables.band_inv))
-
-
-def exchange(x):
-    return lax.all_to_all(x, "pat", split_axis=0, concat_axis=0, tiled=True)
 
 
 def body(slab_phase, pupil_phase, pupil_mask, led_code, led_freq, measured):
@@ -693,49 +814,49 @@
 
     one = Names(**{**vars(dims), **dict(count=1)})
     (y,) = run_rows(
-        "enter", None, "full", one,
+        7, "enter", None, "full", one,
         dict(tr=transmission[0], fwd=table.full, twiddle=twiddle),
         dict(y=(devs, 1, rows, lanes)),
     )
-    x = exchange(run_cols(exchange(y), prop, ct, dims, 1, count, 1.0))
+    x = run_cols(1, y, prop, ct, dims, 1, count, 1.0)
     y, passed1 = run_rows(
-        "forward", "full", "full", dims, dict(x=x, tr=transmission[1], **full_both),
+        8, "forward", "full", "full", dims, dict(x=x, tr=transmission[1], **full_both),
         dict(y=shape_full, passed=shape_field),
     )
-    x = exchange(run_cols(exchange(y), prop, ct, dims, count, count, 1.0))
+    x = run_cols(2, y, prop, ct, dims, count, count, 1.0)
     y, passed2 = run_rows(
-        "forward_band", "full", "band", dims,
+        9, "forward_band", "full", "band", dims,
         dict(x=x, tr=transmission[2], inv=table.full_inv, fwd=table.band, twiddle=twiddle, **tilts),
         dict(y=shape_band, passed=shape_field),
     )
-    x = exchange(run_band(exchange(y), pupil, ct, dims, 1.0))
+    x = run_band(3, y, pupil, ct, dims, 1.0)
     stat_rows = count + count * (count + 1) // 2 + patterns * count + patterns
     dims.stat_rows = stat_rows
     camera, sums = run_rows(
-        "stats", "band", None, dims,
+        10, "stats", "band", None, dims,
         dict(x=x, inv=table.band_inv, twiddle=twiddle, measured=measured),
-        dict(passed=shape_field, sums=(devs, -(-stat_rows // 8) * 8, lanes)),
+        dict(passed=shape_field, y=(devs, -(-stat_rows // 8) * 8, lanes)),
     )
     (y,) = run_rows(
-        "weigh", None, "band", dims,
-        dict(stats=exchange(sums), code=led_code, passed=camera, measured=measured, fwd=table.band, twiddle=twiddle),
+        11, "weigh", None, "band", dims,
+        dict(stats=sums, code=led_code, passed=camera, measured=measured, fwd=table.band, twiddle=twiddle),
         dict(y=shape_band),
     )
-    x = exchange(run_band(exchange(y), pupil, ct, dims, -1.0))
+    x = run_band(4, y, pupil, ct, dims, -1.0)
     y, grad2 = run_rows(
-        "back_band", "band", "full", dims,
+        12, "back_band", "band", "full", dims,
         dict(x=x, tr=transmission[2], passed=passed2, inv=table.band_inv, fwd=table.full, twiddle=twiddle, **tilts),
         dict(y=shape_full, grad=(rows, size)),
     )
-    x = exchange(run_cols(exchange(y), prop, ct, dims, count, count, -1.0))
+    x = run_cols(5, y, prop, ct, dims, count, count, -1.0)
     y, grad1 = run_rows(
-        "back", "full", "full", dims,
+        13, "back", "full", "full", dims,
         dict(x=x, tr=transmission[1], passed=passed1, **full_both),
         dict(y=shape_full, grad=(rows, size)),
     )
-    x = exchange(run_cols(exchange(y), prop, ct, dims, count, 1, -1.0))
+    x = run_cols(6, y, prop, ct, dims, count, 1, -1.0)
     (grad0,) = run_rows(
-        "leave", "full", None, one,
+        14, "leave", "full", None, one,
         dict(x=x, tr=transmission[0], inv=table.full_inv, twiddle=twiddle),
         dict(grad=(rows, size)),
     )

time: 382 us -> 323 us (0.85)
  Pallas kernels: 72.4 us -> 287 us
  blocking collectives: 184 us -> 0 us
  waiting for transfers between devices: 59.2 us -> 0.01 us
  starting transfers between devices: 41.4 us -> 15.7 us
    all_to_all x8 -> x0, blocking collectives: 184 us -> none  [exchange(): return lax.all_to_all(x, 'pat', split_axis=0, concat_axis=0, tiled=True)]
    pallas_call x8, Pallas kernels: 36.6 us -> 147 us  [run_rows(): pl.pallas_call(functools.partial(row_kernel, spec), out_shape=[jax.ShapeD...]
    pallas_call x4, Pallas kernels: 25.5 us -> 117 us  [run_cols(): pl.pallas_call(functools.partial(col_kernel, spec), out_shape=jax.ShapeDt...]
    all_to_all x5 -> x0, waiting for transfers between devices: 57.7 us -> none  [exchange(): return lax.all_to_all(x, 'pat', split_axis=0, concat_axis=0, tiled=True)]
    all_to_all x5 -> x0, starting transfers between devices: 26.9 us -> none  [exchange(): return lax.all_to_all(x, 'pat', split_axis=0, concat_axis=0, tiled=True)]
    pallas_call x2, Pallas kernels: 10.3 us -> 23 us  [run_band(): pl.pallas_call(functools.partial(band_kernel, Names(**vars(dims), sign=si...]
  transfers between devices with their start and end apart: 9 -> 4, of which waited for: 6 -> 0; matrix products, arithmetic and copies ran while one was open for 3% -> 5% of each run, Pallas kernels for 0% -> 38%
where the time goes in v2:
time: 323 us; the launch traced here: 322 us
  Pallas kernels  287 us (89%)
  starting transfers between devices  15.7 us (5%)
  other arithmetic  11.1 us (3%)
  local copies, waits for them, and re-layouts  8.54 us (3%)
    pallas_call x8, Pallas kernels, run_rows(): pl.pallas_call(functools.partial(row_kernel, spec), out_shape=[jax.ShapeD...  147 us
    pallas_call x4, Pallas kernels, run_cols(): pl.pallas_call(functools.partial(col_kernel, spec), out_shape=jax.ShapeDt...  117 us
    pallas_call x2, Pallas kernels, run_band(): pl.pallas_call(functools.partial(band_kernel, Names(**vars(dims), sign=si...  23 us
    ppermute x4, starting transfers between devices, body(): pupil = pupil + lax.ppermute(own[:, :, j], 'pat', pairs)  15.7 us
  transfers between devices with their start and end apart: 4, of which 0 were waited for; matrix products, arithmetic and copies ran while one was open for 5% of the time, Pallas kernels for 38%

profile of v2, /device:TPU:0, one launch (start us, length us, event | category | flops | bytes accessed | tf_op | source)
XLA Modules:
  0.0 322.4 jit_solution(6429264228299706013)
XLA Ops:
  1.9 5.9 %collective-permute-start.1 = (f32[2,16,256]{2,1,0:T(8,128)S(1)}, f32[2,16,256]{2,1,0:T(8,128)S(1)}, u32[]{:S(2)}, u32[]{:S(2)}) collective-permute-start(f32[2,16,256]{2,1,0:T(8,128)S(1)} %get-tuple-element.37), channel_id=1, source_target_pairs={{14,4},{15,5},{0,6},{1,7},{30,20},{31,21},{16,22},{17,23}} | collective-permute-start | bytes 98312 | tf_op jit(solution)/shard_map/ppermute | solution.py:802
  7.8 1.9 collective-permute-start
  9.7 6.6 %collective-permute-start.3 = (f32[2,16,256]{2,1,0:T(8,128)S(1)}, f32[2,16,256]{2,1,0:T(8,128)S(1)}, u32[]{:S(2)}, u32[]{:S(2)}) collective-permute-start(f32[2,16,256]{2,1,0:T(8,128)S(1)} %get-tuple-element.39), channel_id=1, source_target_pairs={{14,12},{15,13},{0,14},{1,15},{30,28},{31,29},{16,30},{17,31}} | collective-permute-start | bytes 98312 | tf_op jit(solution)/shard_map/ppermute | solution.py:802
  16.3 1.3 collective-permute-start.2
  17.7 1.0 slice_reduce_fusion.1
  19.3 3.9 %slice_cosine_fusion = (f32[1,64,1024]{2,1,0:T(8,128)S(1)}, f32[1,64,1024]{2,1,0:T(8,128)S(1)}, f32[1,64,1024]{2,1,0:T(8,128)S(1)}, f32[1,64,1024]{2,1,0:T(8,128...) fusion(f32[3,64,1024]{2,1,0:T(8,128)} %param.15), kind=kLoop, calls=%fused_computation.17 | loop fusion | bytes 2359296 | tf_op jit(solution)/shard_map/cos | solution.py:777
  24.1 4.3 %fusion.1 = (f32[1,2,4,256,128]{4,3,2,1,0:T(8,128)S(1)}, f32[1,2,4,256,128]{4,3,2,1,0:T(8,128)S(1)}) fusion(s32[2,128]{1,0:T(2,128)S(1)} %fusion.28, s32[2,4,256]{2,1,0:T(4,128)S(1)} %fusion.18), kind=kLoop, calls=%fused_computation.4 | loop fusion | flops 2359296 | bytes 2106368 | tf_op jit(solution)/shard_map/jit(_where)/select_n | solution.py:790
  28.4 1.5 pad_maximum_fusion.p_ref
  29.9 1.1 pad_maximum_fusion.2
  32.2 16.1 %rows_enter.1.x_ref = f32[16,1,64,128]{3,2,1,0:T(8,128)} custom-call(f32[2,64,1024]{2,1,0:T(8,128)} %get-tuple-element.49.refs_0_.refs_1_, bf16[2,512,512]{2,1,0:T(8,128)(2,1)} %constant.126.clone.refs_1_.refs_3_.refs_4_, f32[8,256]{1,0:T(8,128)} %constant.130.clone.refs_2_.refs_4_.refs_5_.refs_3_), custom_call_target="tpu_custom_call" | custom-call | tf_op jit(solution)/shard_map/rows_enter/pallas_call | solution.py:593
  48.3 28.8 %cols.4.refs_0_ = f32[16,2,64,128]{3,2,1,0:T(8,128)} custom-call(f32[16,1,64,128]{3,2,1,0:T(8,128)} %rows_enter.1.x_ref, f32[2,2,4,256,128]{4,3,2,1,0:T(8,128)} %pad_maximum_fusion.p_ref, bf16[2,512,256]{2,1,0:T(8,128)(2,1)} %constant.131.clone.w_ref, f32[2,3,256,128]{3,2,1,0:T(8,128)} %constant.132.clone.t_ref), custom_call_target="tpu_custom_call" | custom-call | tf_op jit(solution)/shard_map/cols/pallas_call | solution.py:682
  77.1 28.8 %rows_forward.1 = (f32[16,2,64,128]{3,2,1,0:T(8,128)}, f32[2,128,1024]{2,1,0:T(8,128)}) custom-call(f32[16,2,64,128]{3,2,1,0:T(8,128)} %cols.4.refs_0_, f32[2,64,1024]{2,1,0:T(8,128)} %get-tuple-element.50.refs_1_, bf16[2,512,512]{2,1,0:T(8,128)(2,1)} %constant.127.clone.refs_2_.refs_3_, bf16[2,512,512]{2,1,0:T(8,128)(2,1)} %constant.126.clone.refs_1_.refs_3_.refs_4_, ...), custom_call_target="tpu_custom_call" | custom-call | tf_op jit(solution)/shard_map/rows_forward/pallas_call | solution.py:593
  105.9 33.0 %cols.5.refs_0_ = f32[16,2,64,128]{3,2,1,0:T(8,128)} custom-call(f32[16,2,64,128]{3,2,1,0:T(8,128)} %get-tuple-element.15.x_ref, f32[2,2,4,256,128]{4,3,2,1,0:T(8,128)} %pad_maximum_fusion.p_ref, bf16[2,512,256]{2,1,0:T(8,128)(2,1)} %constant.131.clone.w_ref, f32[2,3,256,128]{3,2,1,0:T(8,128)} %constant.132.clone.t_ref), custom_call_target="tpu_custom_call" | custom-call | tf_op jit(solution)/shard_map/cols/pallas_call | solution.py:682
  139.7 16.1 %rows_forward_band.1 = (f32[16,32,128]{2,1,0:T(8,128)}, f32[2,128,1024]{2,1,0:T(8,128)}) custom-call(f32[16,2,64,128]{3,2,1,0:T(8,128)} %cols.5.refs_0_, f32[2,64,1024]{2,1,0:T(8,128)} %pad_maximum_fusion.4.refs_1_, bf16[2,512,512]{2,1,0:T(8,128)(2,1)} %constant.127.clone.refs_2_.refs_3_, bf16[2,512,128]{2,1,0:T(8,128)(2,1)} %constant.128.clone.refs_3_.refs_4_, ...), custom_call_target="tpu_custom_call" | custom-call | tf_op jit(solution)/shard_map/rows_forward_band/pallas_call | solution.py:593
  156.4 11.1 %pupil_cols.2.refs_0_ = f32[16,32,128]{2,1,0:T(8,128)} custom-call(f32[16,32,128]{2,1,0:T(8,128)} %get-tuple-element.16.x_ref, f32[2,16,256]{2,1,0:T(8,128)} %add_add_fusion.p_ref, bf16[2,1024,512]{2,1,0:T(8,128)(2,1)} %constant.133.clone.w_ref, bf16[2,256,2048]{2,1,0:T(8,128)(2,1)} %constant.134.clone.v_ref), custom_call_target="tpu_custom_call" | custom-call | tf_op jit(solution)/shard_map/pupil_cols/pallas_call | solution.py:749
  167.6 12.4 %rows_stats.1 = (f32[2,128,1024]{2,1,0:T(8,128)}, f32[16,24,128]{2,1,0:T(8,128)}) custom-call(f32[16,32,128]{2,1,0:T(8,128)} %pupil_cols.2.refs_0_, bf16[2,128,512]{2,1,0:T(8,128)(2,1)} %constant.129.clone.refs_1_.refs_3_, f32[8,256]{1,0:T(8,128)} %constant.130.clone.refs_2_.refs_4_.refs_5_.refs_3_, s32[4,64,1024]{2,1,0:T(8,128)} %refs_3_.8), custom_call_target="tpu_custom_call" | custom-call | tf_op jit(solution)/shard_map/rows_stats/pallas_call | solution.py:593
  180.0 13.9 %rows_weigh.1.x_ref = f32[16,32,128]{2,1,0:T(8,128)} custom-call(f32[16,24,128]{2,1,0:T(8,128)} %get-tuple-element.17.refs_0_, s32[4,2]{1,0:T(4,128)} %copy.21.refs_1_, f32[2,128,1024]{2,1,0:T(8,128)} %get-tuple-element.18.refs_2_, s32[4,64,1024]{2,1,0:T(8,128)} %refs_3_.8, bf16[2,512,128]{2,1,0:T(8,128)(2,1)} %constant.128.clone.refs_3_.refs_4_, ...), custom_call_target="tpu_custom_call" | custom-call | tf_op jit(solution)/shard_map/rows_weigh/pallas_call | solution.py:593
  193.9 11.9 %pupil_cols.3.refs_0_ = f32[16,32,128]{2,1,0:T(8,128)} custom-call(f32[16,32,128]{2,1,0:T(8,128)} %rows_weigh.1.x_ref, f32[2,16,256]{2,1,0:T(8,128)} %add_add_fusion.p_ref, bf16[2,1024,512]{2,1,0:T(8,128)(2,1)} %constant.133.clone.w_ref, bf16[2,256,2048]{2,1,0:T(8,128)(2,1)} %constant.134.clone.v_ref), custom_call_target="tpu_custom_call" | custom-call | tf_op jit(solution)/shard_map/pupil_cols/pallas_call | solution.py:749
  205.8 27.6 %rows_back_band.1 = (f32[16,2,64,128]{3,2,1,0:T(8,128)}, f32[64,1024]{1,0:T(8,128)}) custom-call(f32[16,32,128]{2,1,0:T(8,128)} %pupil_cols.3.refs_0_, f32[2,64,1024]{2,1,0:T(8,128)} %pad_maximum_fusion.4.refs_1_, f32[2,128,1024]{2,1,0:T(8,128)} %get-tuple-element.19.refs_2_, bf16[2,128,512]{2,1,0:T(8,128)(2,1)} %constant.129.clone.refs_1_.refs_3_, ...), custom_call_target="tpu_custom_call" | custom-call | tf_op jit(solution)/shard_map/rows_back_band/pallas_call | solution.py:593
  233.4 33.1 %cols.6.refs_0_ = f32[16,2,64,128]{3,2,1,0:T(8,128)} custom-call(f32[16,2,64,128]{3,2,1,0:T(8,128)} %get-tuple-element.20.x_ref, f32[2,2,4,256,128]{4,3,2,1,0:T(8,128)} %pad_maximum_fusion.p_ref, bf16[2,512,256]{2,1,0:T(8,128)(2,1)} %constant.131.clone.w_ref, f32[2,3,256,128]{3,2,1,0:T(8,128)} %constant.132.clone.t_ref), custom_call_target="tpu_custom_call" | custom-call | tf_op jit(solution)/shard_map/cols/pallas_call | solution.py:682
  266.5 28.1 %rows_back.1 = (f32[16,2,64,128]{3,2,1,0:T(8,128)}, f32[64,1024]{1,0:T(8,128)}) custom-call(f32[16,2,64,128]{3,2,1,0:T(8,128)} %cols.6.refs_0_, f32[2,64,1024]{2,1,0:T(8,128)} %get-tuple-element.50.refs_1_, f32[2,128,1024]{2,1,0:T(8,128)} %get-tuple-element.21.refs_2_, bf16[2,512,512]{2,1,0:T(8,128)(2,1)} %constant.127.clone.refs_2_.refs_3_, ...), custom_call_target="tpu_custom_call" | custom-call | tf_op jit(solution)/shard_map/rows_back/pallas_call | solution.py:593
  294.6 22.3 %cols.7.refs_0_ = f32[16,1,64,128]{3,2,1,0:T(8,128)} custom-call(f32[16,2,64,128]{3,2,1,0:T(8,128)} %get-tuple-element.22.x_ref, f32[2,2,4,256,128]{4,3,2,1,0:T(8,128)} %pad_maximum_fusion.p_ref, bf16[2,512,256]{2,1,0:T(8,128)(2,1)} %constant.131.clone.w_ref, f32[2,3,256,128]{3,2,1,0:T(8,128)} %constant.132.clone.t_ref), custom_call_target="tpu_custom_call" | custom-call | tf_op jit(solution)/shard_map/cols/pallas_call | solution.py:682
  316.9 3.6 %rows_leave.1 = f32[64,1024]{1,0:T(8,128)} custom-call(f32[16,1,64,128]{3,2,1,0:T(8,128)} %cols.7.refs_0_, f32[2,64,1024]{2,1,0:T(8,128)} %get-tuple-element.49.refs_0_.refs_1_, bf16[2,512,512]{2,1,0:T(8,128)(2,1)} %constant.127.clone.refs_2_.refs_3_, f32[8,256]{1,0:T(8,128)} %constant.130.clone.refs_2_.refs_4_.refs_5_.refs_3_), custom_call_target="tpu_custom_call" | custom-call | tf_op jit(solution)/shard_map/rows_leave/pallas_call | solution.py:593
  320.5 1.9 pad_maximum_fusion.1
  (33 shorter events, 6.1 us)
Async XLA Ops:
  1.9 153.9 %collective-permute-start.1 = (f32[2,16,256]{2,1,0:T(8,128)S(1)}, f32[2,16,256]{2,1,0:T(8,128)S(1)}, u32[]{:S(2)}, u32[]{:S(2)}) collective-permute-start(f32[2,16,256]{2,1,0:T(8,128)S(1)} %get-tuple-element.37), channel_id=1, source_target_pairs={{14,4},{15,5},{0,6},{1,7},{30,20},{31,21},{16,22},{17,23}} | collective-permute-start | bytes 98312 | tf_op jit(solution)/shard_map/ppermute | solution.py:802
  7.8 148.0 %collective-permute-start = (f32[2,16,256]{2,1,0:T(8,128)S(1)}, f32[2,16,256]{2,1,0:T(8,128)S(1)}, u32[]{:S(2)}, u32[]{:S(2)}) collective-permute-start(f32[2,16,256]{2,1,0:T(8,128)S(1)} %get-tuple-element.38), channel_id=1, source_target_pairs={{14,0},{15,1},{0,2},{1,3},{30,16},{31,17},{16,18},{17,19}} | collective-permute-start | bytes 98312 | tf_op jit(solution)/shard_map/ppermute | solution.py:802
  9.7 146.1 %collective-permute-start.3 = (f32[2,16,256]{2,1,0:T(8,128)S(1)}, f32[2,16,256]{2,1,0:T(8,128)S(1)}, u32[]{:S(2)}, u32[]{:S(2)}) collective-permute-start(f32[2,16,256]{2,1,0:T(8,128)S(1)} %get-tuple-element.39), channel_id=1, source_target_pairs={{14,12},{15,13},{0,14},{1,15},{30,28},{31,29},{16,30},{17,31}} | collective-permute-start | bytes 98312 | tf_op jit(solution)/shard_map/ppermute | solution.py:802
  16.3 139.5 %collective-permute-start.2 = (f32[2,16,256]{2,1,0:T(8,128)S(1)}, f32[2,16,256]{2,1,0:T(8,128)S(1)}, u32[]{:S(2)}, u32[]{:S(2)}) collective-permute-start(f32[2,16,256]{2,1,0:T(8,128)S(1)} %get-tuple-element.40), channel_id=1, source_target_pairs={{14,8},{15,9},{0,10},{1,11},{30,24},{31,25},{16,26},{17,27}} | collective-permute-start | bytes 98312 | tf_op jit(solution)/shard_map/ppermute | solution.py:802
  29.9 1.1 copy-start.2
  316.9 3.6 %copy-start = (f32[64,1024]{1,0:T(8,128)S(1)}, f32[64,1024]{1,0:T(8,128)}, u32[]{:S(2)}) copy-start(f32[64,1024]{1,0:T(8,128)} %get-tuple-element.24) | copy-start | bytes 786436
  316.9 3.6 %copy-start.1 = (f32[64,1024]{1,0:T(8,128)S(1)}, f32[64,1024]{1,0:T(8,128)}, u32[]{:S(2)}) copy-start(f32[64,1024]{1,0:T(8,128)} %get-tuple-element.23) | copy-start | bytes 786436

commit v3 on v2

--- a/solution.py
+++ b/solution.py
@@ -286,50 +286,53 @@
     return me, barrier
 
 
-def remote(ref, me, dest):
-    block = ref.stage if ref.same else ref.stage.at[dest]
+def view(ref, at, part):
+    return ref.at[at] if part is None else ref.at[at, part]
+
+
+def remote(ref, me, dest, part, land):
+    block = ref.stage if ref.same else view(ref.stage, dest, part)
+    row = 0 if part is None else part
     return pltpu.make_async_remote_copy(
-        src_ref=block, dst_ref=ref.y.at[me], send_sem=ref.sent.at[dest],
-        recv_sem=ref.got.at[me], device_id=dict(pat=dest), device_id_type=pl.DeviceIdType.MESH,
-    )
-
-
-def send(ref, me, dest):
+        src_ref=block, dst_ref=view(ref.y, land, part), send_sem=ref.sent.at[row, dest],
+        recv_sem=ref.got.at[row, land], device_id=dict(pat=dest),
+        device_id_type=pl.DeviceIdType.MESH,
+    )
+
+
+def send(ref, me, dest, part=None):
     @pl.when(dest != me)
     def _():
-        remote(ref, me, dest).start()
+        remote(ref, me, dest, part, me).start()
 
     @pl.when(dest == me)
     def _():
-        keep(ref, me).start()
-
-
-def keep(ref, me):
-    block = ref.stage if ref.same else ref.stage.at[me]
-    return pltpu.make_async_copy(block, ref.y.at[me], ref.kept)
-
-
-def finish(ref, me, devs):
-    def settle(step, carry):
-        other = partner(me, step, devs)
-        block = ref.stage if ref.same else ref.stage.at[other]
-        pltpu.make_async_remote_copy(
-            src_ref=block, dst_ref=ref.y.at[other], send_sem=ref.sent.at[other],
-            recv_sem=ref.got.at[other], device_id=dict(pat=other),
-            device_id_type=pl.DeviceIdType.MESH,
-        ).wait()
-        return carry
-
-    keep(ref, me).wait()
-    lax.fori_loop(1, devs, settle, 0)
-
-
-def comm_scratch(stage_shape, devs):
+        keep(ref, me, part).start()
+
+
+def keep(ref, me, part):
+    block = ref.stage if ref.same else view(ref.stage, me, part)
+    return pltpu.make_async_copy(block, view(ref.y, me, part), ref.kept.at[0 if part is None else part])
+
+
+def finish(ref, me, devs, parts=(None,)):
+    for part in parts:
+
+        def settle(step, carry):
+            other = partner(me, step, devs)
+            remote(ref, me, other, part, other).wait()
+            return carry
+
+        keep(ref, me, part).wait()
+        lax.fori_loop(1, devs, settle, 0)
+
+
+def comm_scratch(stage_shape, devs, parts=1):
     return [
         pltpu.VMEM(stage_shape, f32),
-        pltpu.SemaphoreType.DMA((devs,)),
-        pltpu.SemaphoreType.DMA((devs,)),
-        pltpu.SemaphoreType.DMA,
+        pltpu.SemaphoreType.DMA((parts, devs)),
+        pltpu.SemaphoreType.DMA((parts, devs)),
+        pltpu.SemaphoreType.DMA((parts,)),
     ]
 
 
@@ -447,7 +450,13 @@
 
         outgoing = []
         if kind == "enter":
-            outgoing = [[(ref.tr[0, here, c], ref.tr[1, here, c]) for c in cut]]
+            outgoing = [[]]
+            for c in cut:
+                phase = ref.slab[0, here, c]
+                cosine, sine = jnp.cos(phase), jnp.sin(phase)
+                ref.tr0[0, here, c] = cosine
+                ref.tr0[1, here, c] = sine
+                outgoing[0].append((cosine, sine))
         elif kind == "forward" or kind == "forward_band":
             for l in range(count):
                 at = pl.ds(pl.multiple_of(l * rows + base_row, step), step)
@@ -570,7 +579,78 @@
         return carry
 
     lax.fori_loop(0, 4, emit, 0)
+    if kind == "enter":
+        pupil_out(spec, ref, me)
+        prepare(spec, ref, me)
+        pupil_in(spec, ref, me)
     finish(ref, me, devs)
+
+
+def pupil_copy(spec, ref, j, dest):
+    return pltpu.make_async_remote_copy(
+        src_ref=ref.own.at[j], dst_ref=ref.pupil, send_sem=ref.psent.at[j], recv_sem=ref.pgot,
+        device_id=dict(pat=dest), device_id_type=pl.DeviceIdType.MESH,
+    )
+
+
+def pupil_out(spec, ref, me):
+    per = spec.devs // 4
+    for q in range(per):
+
+        @pl.when(me == spec.owners[q])
+        def _():
+            for j in range(4):
+                pupil_copy(spec, ref, j, per * j + q).start()
+
+
+def pupil_in(spec, ref, me):
+    per = spec.devs // 4
+    pupil_copy(spec, ref, 0, partner(me, 1, spec.devs)).wait_recv()
+    for q in range(per):
+
+        @pl.when(me == spec.owners[q])
+        def _():
+            for j in range(4):
+                pupil_copy(spec, ref, j, per * j + q).wait_send()
+
+
+def prepare(spec, ref, me):
+    size, quarter = 4 * spec.quarter, spec.quarter
+    per, half, step = spec.devs // 4, lanes // 2, 16
+    cutoff = size // 2 * (size // 2)
+
+    def phases(i, carry):
+        here = pl.ds(pl.multiple_of(i * step, step), step)
+        for s, out in ((1, ref.tr1), (2, ref.tr2)):
+            phase = ref.slab[s, here, :]
+            out[0, here, :] = jnp.cos(phase)
+            out[1, here, :] = jnp.sin(phase)
+        return carry
+
+    lax.fori_loop(0, spec.rows // step, phases, 0)
+
+    def centred(index):
+        return jnp.where(index >= size // 2, index - size, index)
+
+    def spectrum(i, carry):
+        here = pl.ds(pl.multiple_of(i * step, step), step)
+        row = lax.broadcasted_iota(jnp.int32, (step, lanes), 0) + i * step
+        lane = lax.broadcasted_iota(jnp.int32, (step, lanes), 1)
+        lane = jnp.where(lane < half, lane, lane - half)
+        col = 4 * (lax.rem(me, per) * half + lane) + me // per
+        for l in range(spec.leds):
+            v = centred(col + ref.freq[l, 1])
+            for j in range(4):
+                u = centred(4 * row + j + ref.freq[l, 0])
+                radius = u * u + v * v
+                inside = radius <= cutoff
+                height = jnp.sqrt(jnp.maximum(cutoff - radius, 0).astype(f32))
+                shift = spread_rate * (height - float(size // 2))
+                ref.prop[0, l, j, here, :] = jnp.where(inside, jnp.cos(shift), 0.0)
+                ref.prop[1, l, j, here, :] = jnp.where(inside, jnp.sin(shift), 0.0)
+        return carry
+
+    lax.fori_loop(0, quarter // step, spectrum, 0)
 
 
 def run_rows(channel, kind, source, target, dims, inputs, outputs):
@@ -585,16 +665,19 @@
         names += ["stage", "sent", "got", "kept"]
         shape = outputs["y"]
         comm = comm_scratch(shape[1:] if kind == "stats" else shape, spec.devs)
+    if kind == "enter":
+        names += ["psent", "pgot"]
+        comm += [pltpu.SemaphoreType.DMA((4,)), pltpu.SemaphoreType.DMA]
     spec.names = names
     vmem = pl.BlockSpec(memory_space=pltpu.VMEM)
     in_specs = [
-        pl.BlockSpec(memory_space=pltpu.SMEM) if name == "code" else vmem for name in inputs
+        pl.BlockSpec(memory_space=pltpu.SMEM) if name in ("code", "freq") else vmem for name in inputs
     ]
     return pl.pallas_call(
         functools.partial(row_kernel, spec),
         out_shape=[jax.ShapeDtypeStruct(shape, f32) for shape in outputs.values()],
         in_specs=in_specs,
-        out_specs=[anywhere if name == "y" else vmem for name in outputs],
+        out_specs=[anywhere if name in ("y", "pupil") else vmem for name in outputs],
         scratch_shapes=[
             pltpu.VMEM((4, total, wide), bf16),
             pltpu.VMEM((4, total, wide), bf16),
@@ -614,64 +697,84 @@
     count = p_ref.shape[1]
     per = devs // 4
     weights = (w_ref[0], w_ref[1])
-
-    def spread(i, carry):
-        here = pl.ds(pl.multiple_of(i * rows, rows), rows)
-        for l in range(count_in):
+    wide_out = count_out * lanes
+
+    def spread(l):
+        at = slice(l * lanes, (l + 1) * lanes)
+
+        def step(i, carry):
+            here = pl.ds(pl.multiple_of(i * rows, rows), rows)
             x0, x1, x2, x3 = [x_ref[per * a + i, l] for a in range(4)]
             s, t, d, e = x0 + x2, x1 + x3, x0 - x2, turn(x1 - x3)
             for j, value in enumerate((s + t, d + e, s - t, d - e)):
                 if j:
                     value = value * t_ref[0, j - 1, here, :] + turn(value) * t_ref[1, j - 1, here, :]
                 high, low = split(value)
-                hi[j, here, l * lanes : (l + 1) * lanes] = high
-                lo[j, here, l * lanes : (l + 1) * lanes] = low
-        return carry
-
-    lax.fori_loop(0, per, spread, 0)
-    wide_in, wide_out = count_in * lanes, count_out * lanes
-    for j in range(4):
-        y = dot3(weights, (hi[j, :, :wide_in], lo[j, :, :wide_in]))
-        spectra = []
-        for l in range(count_in):
-            at = slice(l * lanes, (l + 1) * lanes)
-            spectra.append(y[:quarter, at] + turn(y[quarter:, at]))
-        results = []
-        for l in range(count):
-            z = spectra[l if count_in > 1 else 0]
-            results.append(z * p_ref[0, l, j] - sign * (turn(z) * p_ref[1, l, j]))
-        if count_out == 1:
-            results = [sum(results)]
-        for l in range(count_out):
-            high, low = split(results[l])
-            hi[j, :, l * lanes : (l + 1) * lanes] = high
-            lo[j, :, l * lanes : (l + 1) * lanes] = low
-    for j in range(4):
-        y = dot3(weights, (hi[j, :, :wide_out], lo[j, :, :wide_out]))
-        for l in range(count_out):
-            at = slice(l * lanes, (l + 1) * lanes)
-            value = y[:quarter, at] - turn(y[quarter:, at])
+                hi[j, here, at] = high
+                lo[j, here, at] = low
+            return carry
+
+        lax.fori_loop(0, per, step, 0)
+
+    def spectra(first, number):
+        span = slice(first * lanes, (first + number) * lanes)
+        found = []
+        for j in range(4):
+            y = dot3(weights, (hi[j, :, span], lo[j, :, span]))
+            found.append([])
+            for l in range(number):
+                at = slice(l * lanes, (l + 1) * lanes)
+                found[j].append(y[:quarter, at] + turn(y[quarter:, at]))
+        return found
+
+    def pass_on(l, fields):
+        at = slice(l * lanes, (l + 1) * lanes)
+        for j in range(4):
+            high, low = split(fields[j])
+            hi[j, :, at] = high
+            lo[j, :, at] = low
+        for j in range(4):
+            y = dot3(weights, (hi[j, :, at], lo[j, :, at]))
+            value = y[:quarter] - turn(y[quarter:])
             if j:
                 value = value * t_ref[0, j - 1] - turn(value) * t_ref[1, j - 1]
             zs[j, :, at] = value
-
-    pl.semaphore_wait(barrier, devs - 1)
-
-    def gather(step, carry):
-        i = lax.rem(me + step, per)
-        here = pl.ds(pl.multiple_of(i * rows, rows), rows)
-        for l in range(count_out):
-            at = slice(l * lanes, (l + 1) * lanes)
+        if l == 0:
+            pl.semaphore_wait(barrier, devs - 1)
+
+        def gather(step, carry):
+            i = lax.rem(me + step, per)
+            here = pl.ds(pl.multiple_of(i * rows, rows), rows)
             g0, g1, g2, g3 = [zs[j, here, at] for j in range(4)]
             s, t, d, e = g0 + g2, g1 + g3, g0 - g2, turn(g1 - g3)
             for a, value in enumerate((s + t, d - e, s - t, d + e)):
                 stage[per * a + i, l] = value
-        for a in range(4):
-            send(ref, me, lax.rem(me // per + a, 4) * per + i)
-        return carry
-
-    lax.fori_loop(0, per, gather, 0)
-    finish(ref, me, devs)
+            for a in range(4):
+                send(ref, me, lax.rem(me // per + a, 4) * per + i, l)
+            return carry
+
+        lax.fori_loop(0, per, gather, 0)
+
+    def shaped(z, l, j):
+        return z * p_ref[0, l, j] - sign * (turn(z) * p_ref[1, l, j])
+
+    if count_in == count_out:
+        for l in range(count):
+            spread(l)
+            z = spectra(l, 1)
+            pass_on(l, [shaped(z[j][0], l, j) for j in range(4)])
+    else:
+        for l in range(count_in):
+            spread(l)
+        z = spectra(0, count_in)
+        if count_out == 1:
+            pass_on(0, [sum(shaped(z[j][l], l, j) for l in range(count)) for j in range(4)])
+        else:
+            for j in range(4):
+                zs[j, :, wide_out:] = z[j][0]
+            for l in range(count):
+                pass_on(l, [shaped(zs[j, :, wide_out:], l, j) for j in range(4)])
+    finish(ref, me, devs, tuple(range(count_out)))
 
 
 def run_cols(channel, x, prop, tables, dims, count_in, count_out, sign):
@@ -687,9 +790,9 @@
         scratch_shapes=[
             pltpu.VMEM((4, quarter, wide), bf16),
             pltpu.VMEM((4, quarter, wide), bf16),
-            pltpu.VMEM((4, quarter, wide), f32),
+            pltpu.VMEM((4, quarter, wide + lanes), f32),
         ]
-        + comm_scratch((devs, count_out, rows, lanes), devs),
+        + comm_scratch((devs, count_out, rows, lanes), devs, count_out),
         compiler_params=comm_params(channel),
         name="cols",
     )(x, prop, jnp.asarray(tables.both), jnp.asarray(tables.twiddle))
@@ -774,32 +877,15 @@
     shape_full = (devs, count, rows, lanes)
     shape_band = (devs, 2 * band_cols, count * rows)
     shape_field = (2, count * rows, size)
-    transmission = [jnp.stack([jnp.cos(slab_phase[s]), jnp.sin(slab_phase[s])]) for s in range(slab_count)]
     twiddle, table = rt.twiddle, rt
-
-    lane = jnp.arange(lanes, dtype=jnp.int32) % cols
-    col_index = 4 * ((position % per) * cols + lane) + position // per
-    row_index = 4 * jnp.arange(quarter, dtype=jnp.int32)[None, :] + jnp.arange(4, dtype=jnp.int32)[:, None]
-    col_freq = frequency(col_index[None, :] + led_freq[:, 1][:, None] + size, size)
-    row_freq = frequency(row_index[None] + led_freq[:, 0][:, None, None] + size, size)
-    radius = (row_freq * row_freq)[..., None] + (col_freq * col_freq)[:, None, None, :]
-    cutoff = size // 2 * (size // 2)
-    inside = radius <= cutoff
-    height = jnp.sqrt(jnp.maximum(cutoff - radius, 0).astype(f32))
-    shift = spread_rate * (height - size // 2)
-    prop = jnp.stack([jnp.where(inside, jnp.cos(shift), 0.0), jnp.where(inside, jnp.sin(shift), 0.0)])
 
     def near(x):
         return jnp.concatenate([x[:, size - pupil_radius :], x[:, :pupil_radius]], 1)
 
     opening, phase = near(pupil_mask).astype(f32), near(pupil_phase)
     own = jnp.stack([opening * jnp.cos(phase), opening * jnp.sin(phase)])
-    own = own.reshape(2, cols // 4, 4, band)
-    pupil = 0.0
+    own = jnp.transpose(own.reshape(2, cols // 4, 4, band), (2, 0, 1, 3))
     owners = [(q - pupil_radius // cols) % devs for q in range(per)]
-    for j in range(4):
-        pairs = [(owners[q], per * j + q) for q in range(per)]
-        pupil = pupil + lax.ppermute(own[:, :, j], "pat", pairs)
 
     def wave(freq, index):
         turns = (freq[:, None] * index[None, :]) % size
@@ -812,12 +898,17 @@
     tilts = dict(tilt_r=tilt_r, tilt_c=tilt_c)
     full_both = dict(inv=table.full_inv, fwd=table.full, twiddle=twiddle)
 
-    one = Names(**{**vars(dims), **dict(count=1)})
-    (y,) = run_rows(
+    one = Names(**{**vars(dims), **dict(count=1)}, leds=count, owners=owners)
+    shape_trans = (2, rows, size)
+    y, tr0, tr1, tr2, prop, pupil = run_rows(
         7, "enter", None, "full", one,
-        dict(tr=transmission[0], fwd=table.full, twiddle=twiddle),
-        dict(y=(devs, 1, rows, lanes)),
-    )
+        dict(slab=slab_phase, own=own, freq=led_freq, fwd=table.full, twiddle=twiddle),
+        dict(
+            y=(devs, 1, rows, lanes), tr0=shape_trans, tr1=shape_trans, tr2=shape_trans,
+            prop=(2, count, 4, quarter, lanes), pupil=(2, band_cols, band),
+        ),
+    )
+    transmission = [tr0, tr1, tr2]
     x = run_cols(1, y, prop, ct, dims, 1, count, 1.0)
     y, passed1 = run_rows(
         8, "forward", "full", "full", dims, dict(x=x, tr=transmission[1], **full_both),

time: 323 us -> 303 us (0.938)
  starting transfers between devices: 15.7 us -> 0 us
  other arithmetic: 11.1 us -> 3.3 us
  Pallas kernels: 287 us -> 293 us
    ppermute x4 -> x0, starting transfers between devices: 15.7 us -> none  [body(): pupil = pupil + lax.ppermute(own[:, :, j], 'pat', pairs)]
    select_n x1 -> x0, other arithmetic: 4.25 us -> none  [body(): jnp.where(inside, jnp.cos(shift), 0.0)]
    cos x1 -> x0, local copies, waits for them, and re-layouts: 3.92 us -> none  [body(): jnp.cos(slab_phase[s])]
    pallas_call x4, Pallas kernels: 117 us -> 121 us  [run_cols(): pl.pallas_call(functools.partial(col_kernel, spec), out_shape=jax.ShapeDt...]
    another operation x3 -> x0, other arithmetic: 3.35 us -> none  [the longest x2 1.88 us: body(): jnp.stack([jnp.cos(slab_phase[s]), jnp.sin(slab_phase[s])])]
  transfers between devices with their start and end apart: 4 -> 0, of which waited for: 0 -> 0; matrix products, arithmetic and copies ran while one was open for 5% -> 0% of each run, Pallas kernels for 38% -> 0%
where the time goes in v3:
time: 303 us; the launch traced here: 302 us
  Pallas kernels  293 us (97%)
  local copies, waits for them, and re-layouts  5.32 us (2%)
  other arithmetic  3.3 us (1%)
    pallas_call x8, Pallas kernels, run_rows(): pl.pallas_call(functools.partial(row_kernel, spec), out_shape=[jax.ShapeD...  149 us
    pallas_call x4, Pallas kernels, run_cols(): pl.pallas_call(functools.partial(col_kernel, spec), out_shape=jax.ShapeDt...  121 us
    pallas_call x2, Pallas kernels, run_band(): pl.pallas_call(functools.partial(band_kernel, Names(**vars(dims), sign=si...  23.2 us

profile of v3, /device:TPU:0, one launch (start us, length us, event | category | flops | bytes accessed | tf_op | source)
XLA Modules:
  0.0 301.7 jit_solution(10894666946068737217)
XLA Ops:
  0.0 1.0 slice_reduce_fusion
  1.1 1.3 copy.21.refs_1_
  2.5 0.3 fusion.4
  2.8 0.6 reshape.371.refs_6_.refs_7_
  3.5 0.8 fusion.11
  4.3 0.8 fusion.10
  5.1 0.2 cosine_multiply_fusion
  5.3 0.7 maximum_bitcast_fusion.refs_1_
  6.0 0.8 broadcast_in_dim.10.refs_5_.refs_6_
  6.8 22.8 %rows_enter.1 = (f32[16,1,64,128]{3,2,1,0:T(8,128)}, f32[2,64,1024]{2,1,0:T(8,128)}, f32[2,64,1024]{2,1,0:T(8,128)}, f32[2,64,1024]{2,1,0:T(8,128)}, f32[2,2,4,2...) custom-call(f32[3,64,1024]{2,1,0:T(8,128)} %refs_0_.1, f32[4,2,16,256]{3,2,1,0:T(8,128)} %maximum_bitcast_fusion.refs_1_, ...), custom_call_target="tpu_custom_call" | custom-call | tf_op jit(solution)/shard_map/rows_enter/pallas_call | solution.py:676
  29.6 30.7 %cols.4.refs_0_ = f32[16,2,64,128]{3,2,1,0:T(8,128)} custom-call(f32[16,1,64,128]{3,2,1,0:T(8,128)} %get-tuple-element.21.x_ref, f32[2,2,4,256,128]{4,3,2,1,0:T(8,128)} %get-tuple-element.22.p_ref, bf16[2,512,256]{2,1,0:T(8,128)(2,1)} %constant.55.clone.w_ref, f32[2,3,256,128]{3,2,1,0:T(8,128)} %constant.56.clone.t_ref), custom_call_target="tpu_custom_call" | custom-call | tf_op jit(solution)/shard_map/cols/pallas_call | solution.py:785
  60.3 26.8 %rows_forward.1 = (f32[16,2,64,128]{3,2,1,0:T(8,128)}, f32[2,128,1024]{2,1,0:T(8,128)}) custom-call(f32[16,2,64,128]{3,2,1,0:T(8,128)} %cols.4.refs_0_, f32[2,64,1024]{2,1,0:T(8,128)} %get-tuple-element.23.refs_1_, bf16[2,512,512]{2,1,0:T(8,128)(2,1)} %constant.51.clone.refs_2_.refs_3_, bf16[2,512,512]{2,1,0:T(8,128)(2,1)} %constant.50.clone.refs_3_.refs_4_, ...), custom_call_target="tpu_custom_call" | custom-call | tf_op jit(solution)/shard_map/rows_forward/pallas_call | solution.py:676
  87.1 34.0 %cols.5.refs_0_ = f32[16,2,64,128]{3,2,1,0:T(8,128)} custom-call(f32[16,2,64,128]{3,2,1,0:T(8,128)} %get-tuple-element.24.x_ref, f32[2,2,4,256,128]{4,3,2,1,0:T(8,128)} %get-tuple-element.22.p_ref, bf16[2,512,256]{2,1,0:T(8,128)(2,1)} %constant.55.clone.w_ref, f32[2,3,256,128]{3,2,1,0:T(8,128)} %constant.56.clone.t_ref), custom_call_target="tpu_custom_call" | custom-call | tf_op jit(solution)/shard_map/cols/pallas_call | solution.py:785
  121.1 14.7 %rows_forward_band.1 = (f32[16,32,128]{2,1,0:T(8,128)}, f32[2,128,1024]{2,1,0:T(8,128)}) custom-call(f32[16,2,64,128]{3,2,1,0:T(8,128)} %cols.5.refs_0_, f32[2,64,1024]{2,1,0:T(8,128)} %get-tuple-element.25.refs_1_, bf16[2,512,512]{2,1,0:T(8,128)(2,1)} %constant.51.clone.refs_2_.refs_3_, bf16[2,512,128]{2,1,0:T(8,128)(2,1)} %constant.52.clone.refs_3_.refs_4_, ...), custom_call_target="tpu_custom_call" | custom-call | tf_op jit(solution)/shard_map/rows_forward_band/pallas_call | solution.py:676
  135.8 11.4 %pupil_cols.2.refs_0_ = f32[16,32,128]{2,1,0:T(8,128)} custom-call(f32[16,32,128]{2,1,0:T(8,128)} %get-tuple-element.26.x_ref, f32[2,16,256]{2,1,0:T(8,128)} %get-tuple-element.27.p_ref, bf16[2,1024,512]{2,1,0:T(8,128)(2,1)} %constant.57.clone.w_ref, bf16[2,256,2048]{2,1,0:T(8,128)(2,1)} %constant.58.clone.v_ref), custom_call_target="tpu_custom_call" | custom-call | tf_op jit(solution)/shard_map/pupil_cols/pallas_call | solution.py:852
  147.1 12.4 %rows_stats.1 = (f32[2,128,1024]{2,1,0:T(8,128)}, f32[16,24,128]{2,1,0:T(8,128)}) custom-call(f32[16,32,128]{2,1,0:T(8,128)} %pupil_cols.2.refs_0_, bf16[2,128,512]{2,1,0:T(8,128)(2,1)} %constant.53.clone.refs_1_.refs_3_, f32[8,256]{1,0:T(8,128)} %constant.54.clone.refs_4_.refs_2_.refs_5_.refs_3_, s32[4,64,1024]{2,1,0:T(8,128)} %refs_3_.9), custom_call_target="tpu_custom_call" | custom-call | tf_op jit(solution)/shard_map/rows_stats/pallas_call | solution.py:676
  159.5 13.9 %rows_weigh.1.x_ref = f32[16,32,128]{2,1,0:T(8,128)} custom-call(f32[16,24,128]{2,1,0:T(8,128)} %get-tuple-element.28.refs_0_, s32[4,2]{1,0:T(4,128)} %copy.21.refs_1_, f32[2,128,1024]{2,1,0:T(8,128)} %get-tuple-element.29.refs_2_, s32[4,64,1024]{2,1,0:T(8,128)} %refs_3_.9, bf16[2,512,128]{2,1,0:T(8,128)(2,1)} %constant.52.clone.refs_3_.refs_4_, ...), custom_call_target="tpu_custom_call" | custom-call | tf_op jit(solution)/shard_map/rows_weigh/pallas_call | solution.py:676
  173.4 11.8 %pupil_cols.3.refs_0_ = f32[16,32,128]{2,1,0:T(8,128)} custom-call(f32[16,32,128]{2,1,0:T(8,128)} %rows_weigh.1.x_ref, f32[2,16,256]{2,1,0:T(8,128)} %get-tuple-element.27.p_ref, bf16[2,1024,512]{2,1,0:T(8,128)(2,1)} %constant.57.clone.w_ref, bf16[2,256,2048]{2,1,0:T(8,128)(2,1)} %constant.58.clone.v_ref), custom_call_target="tpu_custom_call" | custom-call | tf_op jit(solution)/shard_map/pupil_cols/pallas_call | solution.py:852
  185.3 27.6 %rows_back_band.1 = (f32[16,2,64,128]{3,2,1,0:T(8,128)}, f32[64,1024]{1,0:T(8,128)}) custom-call(f32[16,32,128]{2,1,0:T(8,128)} %pupil_cols.3.refs_0_, f32[2,64,1024]{2,1,0:T(8,128)} %get-tuple-element.25.refs_1_, f32[2,128,1024]{2,1,0:T(8,128)} %get-tuple-element.30.refs_2_, bf16[2,128,512]{2,1,0:T(8,128)(2,1)} %constant.53.clone.refs_1_.refs_3_, ...), custom_call_target="tpu_custom_call" | custom-call | tf_op jit(solution)/shard_map/rows_back_band/pallas_call | solution.py:676
  212.9 34.1 %cols.6.refs_0_ = f32[16,2,64,128]{3,2,1,0:T(8,128)} custom-call(f32[16,2,64,128]{3,2,1,0:T(8,128)} %get-tuple-element.31.x_ref, f32[2,2,4,256,128]{4,3,2,1,0:T(8,128)} %get-tuple-element.22.p_ref, bf16[2,512,256]{2,1,0:T(8,128)(2,1)} %constant.55.clone.w_ref, f32[2,3,256,128]{3,2,1,0:T(8,128)} %constant.56.clone.t_ref), custom_call_target="tpu_custom_call" | custom-call | tf_op jit(solution)/shard_map/cols/pallas_call | solution.py:785
  247.0 27.0 %rows_back.1 = (f32[16,2,64,128]{3,2,1,0:T(8,128)}, f32[64,1024]{1,0:T(8,128)}) custom-call(f32[16,2,64,128]{3,2,1,0:T(8,128)} %cols.6.refs_0_, f32[2,64,1024]{2,1,0:T(8,128)} %get-tuple-element.23.refs_1_, f32[2,128,1024]{2,1,0:T(8,128)} %get-tuple-element.32.refs_2_, bf16[2,512,512]{2,1,0:T(8,128)(2,1)} %constant.51.clone.refs_2_.refs_3_, ...), custom_call_target="tpu_custom_call" | custom-call | tf_op jit(solution)/shard_map/rows_back/pallas_call | solution.py:676
  274.0 22.2 %cols.7.refs_0_ = f32[16,1,64,128]{3,2,1,0:T(8,128)} custom-call(f32[16,2,64,128]{3,2,1,0:T(8,128)} %get-tuple-element.33.x_ref, f32[2,2,4,256,128]{4,3,2,1,0:T(8,128)} %get-tuple-element.22.p_ref, bf16[2,512,256]{2,1,0:T(8,128)(2,1)} %constant.55.clone.w_ref, f32[2,3,256,128]{3,2,1,0:T(8,128)} %constant.56.clone.t_ref), custom_call_target="tpu_custom_call" | custom-call | tf_op jit(solution)/shard_map/cols/pallas_call | solution.py:785
  296.2 3.6 %rows_leave.1 = f32[64,1024]{1,0:T(8,128)} custom-call(f32[16,1,64,128]{3,2,1,0:T(8,128)} %cols.7.refs_0_, f32[2,64,1024]{2,1,0:T(8,128)} %get-tuple-element.34.refs_1_, bf16[2,512,512]{2,1,0:T(8,128)(2,1)} %constant.51.clone.refs_2_.refs_3_, f32[8,256]{1,0:T(8,128)} %constant.54.clone.refs_4_.refs_2_.refs_5_.refs_3_), custom_call_target="tpu_custom_call" | custom-call | tf_op jit(solution)/shard_map/rows_leave/pallas_call | solution.py:676
  299.8 1.9 pad_maximum_fusion
  (12 shorter events, 0.2 us)
Async XLA Ops:
  296.2 3.6 %copy-start = (f32[64,1024]{1,0:T(8,128)S(1)}, f32[64,1024]{1,0:T(8,128)}, u32[]{:S(2)}) copy-start(f32[64,1024]{1,0:T(8,128)} %get-tuple-element.36) | copy-start | bytes 786436
  296.2 3.6 %copy-start.1 = (f32[64,1024]{1,0:T(8,128)S(1)}, f32[64,1024]{1,0:T(8,128)}, u32[]{:S(2)}) copy-start(f32[64,1024]{1,0:T(8,128)} %get-tuple-element.35) | copy-start | bytes 786436

commit v4 on v3

--- a/solution.py
+++ b/solution.py
@@ -308,6 +308,22 @@
     @pl.when(dest == me)
     def _():
         keep(ref, me, part).start()
+
+
+def groups(me, per):
+    z = me // per
+    return [lax.rem(z + 2, 4), 3 - z, z + 1 - 2 * lax.rem(z, 2), z]
+
+
+def send_all(ref, me, devs, part=None):
+    per = devs // 4
+    for j in groups(me, per):
+
+        def share(q, carry):
+            send(ref, me, per * j + lax.rem(me + q, per), part)
+            return carry
+
+        lax.fori_loop(0, per, share, 0)
 
 
 def keep(ref, me, part):
@@ -550,12 +566,7 @@
         packed = jnp.concatenate(packed, 0)
         ref.stage[...] = packed
         pl.semaphore_wait(barrier, devs - 1)
-
-        def share(k, carry):
-            send(ref, me, partner(me, k, devs))
-            return carry
-
-        lax.fori_loop(0, devs, share, 0)
+        send_all(ref, me, devs)
         finish(ref, me, devs)
         return
     lax.fori_loop(0, rows // step, chunk, 0)
@@ -563,8 +574,7 @@
         return
     pl.semaphore_wait(barrier, devs - 1)
 
-    def emit(step_j, carry):
-        j = lax.rem(me // per + step_j, 4)
+    def emit(j):
         y = dot3((hi[j, :total, :], lo[j, :total, :]), (ref.fwd[0], ref.fwd[1]))
         if spec.target == "full":
             for q in range(per):
@@ -576,9 +586,9 @@
                 ref.stage[per * j + q] = flipped[q * deep : (q + 1) * deep]
         for q in range(per):
             send(ref, me, per * j + lax.rem(me + q, per))
-        return carry
-
-    lax.fori_loop(0, 4, emit, 0)
+
+    for j in groups(me, per):
+        emit(j)
     if kind == "enter":
         pupil_out(spec, ref, me)
         prepare(spec, ref, me)
@@ -749,11 +759,10 @@
             s, t, d, e = g0 + g2, g1 + g3, g0 - g2, turn(g1 - g3)
             for a, value in enumerate((s + t, d - e, s - t, d + e)):
                 stage[per * a + i, l] = value
-            for a in range(4):
-                send(ref, me, lax.rem(me // per + a, 4) * per + i, l)
             return carry
 
         lax.fori_loop(0, per, gather, 0)
+        send_all(ref, me, devs, l)
 
     def shaped(z, l, j):
         return z * p_ref[0, l, j] - sign * (turn(z) * p_ref[1, l, j])
@@ -838,12 +847,7 @@
         stage[s] = jnp.where(lane < half, first, pltpu.roll(second, half, 1))
         stage[s + 1] = jnp.where(lane < half, pltpu.roll(first, half, 1), second)
     pl.semaphore_wait(barrier, devs - 1)
-
-    def share(k, carry):
-        send(ref, me, partner(me, k, devs))
-        return carry
-
-    lax.fori_loop(0, devs, share, 0)
+    send_all(ref, me, devs)
     finish(ref, me, devs)
 
 

time: 303 us -> 296 us (0.977)
  Pallas kernels: 293 us -> 287 us
    pallas_call x8, Pallas kernels: 149 us -> 143 us  [run_rows(): pl.pallas_call(functools.partial(row_kernel, spec), out_shape=[jax.ShapeD...]
where the time goes in v4:
time: 296 us; the launch traced here: 295 us
  Pallas kernels  287 us (97%)
  local copies, waits for them, and re-layouts  5.3 us (2%)
  other arithmetic  3.3 us (1%)
    pallas_call x8, Pallas kernels, run_rows(): pl.pallas_call(functools.partial(row_kernel, spec), out_shape=[jax.ShapeD...  143 us
    pallas_call x4, Pallas kernels, run_cols(): pl.pallas_call(functools.partial(col_kernel, spec), out_shape=jax.ShapeDt...  118 us
    pallas_call x2, Pallas kernels, run_band(): pl.pallas_call(functools.partial(band_kernel, Names(**vars(dims), sign=si...  25.6 us

profile of v4, /device:TPU:0, one launch (start us, length us, event | category | flops | bytes accessed | tf_op | source)
XLA Modules:
  0.0 295.4 jit_solution(5029633020345230293)
XLA Ops:
  0.0 1.0 slice_reduce_fusion
  1.1 1.3 copy.21.refs_1_
  2.5 0.3 fusion.4
  2.8 0.6 reshape.371.refs_6_.refs_7_
  3.5 0.8 fusion.11
  4.3 0.8 fusion.10
  5.1 0.2 cosine_multiply_fusion
  5.3 0.7 maximum_bitcast_fusion.refs_1_
  6.0 0.8 broadcast_in_dim.10.refs_5_.refs_6_
  6.8 22.4 %rows_enter.1 = (f32[16,1,64,128]{3,2,1,0:T(8,128)}, f32[2,64,1024]{2,1,0:T(8,128)}, f32[2,64,1024]{2,1,0:T(8,128)}, f32[2,64,1024]{2,1,0:T(8,128)}, f32[2,2,4,2...) custom-call(f32[3,64,1024]{2,1,0:T(8,128)} %refs_0_.1, f32[4,2,16,256]{3,2,1,0:T(8,128)} %maximum_bitcast_fusion.refs_1_, ...), custom_call_target="tpu_custom_call" | custom-call | tf_op jit(solution)/shard_map/rows_enter/pallas_call | solution.py:686
  29.2 29.3 %cols.4.refs_0_ = f32[16,2,64,128]{3,2,1,0:T(8,128)} custom-call(f32[16,1,64,128]{3,2,1,0:T(8,128)} %get-tuple-element.21.x_ref, f32[2,2,4,256,128]{4,3,2,1,0:T(8,128)} %get-tuple-element.22.p_ref, bf16[2,512,256]{2,1,0:T(8,128)(2,1)} %constant.55.clone.w_ref, f32[2,3,256,128]{3,2,1,0:T(8,128)} %constant.56.clone.t_ref), custom_call_target="tpu_custom_call" | custom-call | tf_op jit(solution)/shard_map/cols/pallas_call | solution.py:794
  58.5 27.0 %rows_forward.1 = (f32[16,2,64,128]{3,2,1,0:T(8,128)}, f32[2,128,1024]{2,1,0:T(8,128)}) custom-call(f32[16,2,64,128]{3,2,1,0:T(8,128)} %cols.4.refs_0_, f32[2,64,1024]{2,1,0:T(8,128)} %get-tuple-element.23.refs_1_, bf16[2,512,512]{2,1,0:T(8,128)(2,1)} %constant.51.clone.refs_2_.refs_3_, bf16[2,512,512]{2,1,0:T(8,128)(2,1)} %constant.50.clone.refs_3_.refs_4_, ...), custom_call_target="tpu_custom_call" | custom-call | tf_op jit(solution)/shard_map/rows_forward/pallas_call | solution.py:686
  85.6 33.0 %cols.5.refs_0_ = f32[16,2,64,128]{3,2,1,0:T(8,128)} custom-call(f32[16,2,64,128]{3,2,1,0:T(8,128)} %get-tuple-element.24.x_ref, f32[2,2,4,256,128]{4,3,2,1,0:T(8,128)} %get-tuple-element.22.p_ref, bf16[2,512,256]{2,1,0:T(8,128)(2,1)} %constant.55.clone.w_ref, f32[2,3,256,128]{3,2,1,0:T(8,128)} %constant.56.clone.t_ref), custom_call_target="tpu_custom_call" | custom-call | tf_op jit(solution)/shard_map/cols/pallas_call | solution.py:794
  118.6 15.2 %rows_forward_band.1 = (f32[16,32,128]{2,1,0:T(8,128)}, f32[2,128,1024]{2,1,0:T(8,128)}) custom-call(f32[16,2,64,128]{3,2,1,0:T(8,128)} %cols.5.refs_0_, f32[2,64,1024]{2,1,0:T(8,128)} %get-tuple-element.25.refs_1_, bf16[2,512,512]{2,1,0:T(8,128)(2,1)} %constant.51.clone.refs_2_.refs_3_, bf16[2,512,128]{2,1,0:T(8,128)(2,1)} %constant.52.clone.refs_3_.refs_4_, ...), custom_call_target="tpu_custom_call" | custom-call | tf_op jit(solution)/shard_map/rows_forward_band/pallas_call | solution.py:686
  133.8 13.0 %pupil_cols.2.refs_0_ = f32[16,32,128]{2,1,0:T(8,128)} custom-call(f32[16,32,128]{2,1,0:T(8,128)} %get-tuple-element.26.x_ref, f32[2,16,256]{2,1,0:T(8,128)} %get-tuple-element.27.p_ref, bf16[2,1024,512]{2,1,0:T(8,128)(2,1)} %constant.57.clone.w_ref, bf16[2,256,2048]{2,1,0:T(8,128)(2,1)} %constant.58.clone.v_ref), custom_call_target="tpu_custom_call" | custom-call | tf_op jit(solution)/shard_map/pupil_cols/pallas_call | solution.py:856
  146.8 11.3 %rows_stats.1 = (f32[2,128,1024]{2,1,0:T(8,128)}, f32[16,24,128]{2,1,0:T(8,128)}) custom-call(f32[16,32,128]{2,1,0:T(8,128)} %pupil_cols.2.refs_0_, bf16[2,128,512]{2,1,0:T(8,128)(2,1)} %constant.53.clone.refs_1_.refs_3_, f32[8,256]{1,0:T(8,128)} %constant.54.clone.refs_4_.refs_2_.refs_5_.refs_3_, s32[4,64,1024]{2,1,0:T(8,128)} %refs_3_.9), custom_call_target="tpu_custom_call" | custom-call | tf_op jit(solution)/shard_map/rows_stats/pallas_call | solution.py:686
  158.1 11.9 %rows_weigh.1.x_ref = f32[16,32,128]{2,1,0:T(8,128)} custom-call(f32[16,24,128]{2,1,0:T(8,128)} %get-tuple-element.28.refs_0_, s32[4,2]{1,0:T(4,128)} %copy.21.refs_1_, f32[2,128,1024]{2,1,0:T(8,128)} %get-tuple-element.29.refs_2_, s32[4,64,1024]{2,1,0:T(8,128)} %refs_3_.9, bf16[2,512,128]{2,1,0:T(8,128)(2,1)} %constant.52.clone.refs_3_.refs_4_, ...), custom_call_target="tpu_custom_call" | custom-call | tf_op jit(solution)/shard_map/rows_weigh/pallas_call | solution.py:686
  170.0 12.6 %pupil_cols.3.refs_0_ = f32[16,32,128]{2,1,0:T(8,128)} custom-call(f32[16,32,128]{2,1,0:T(8,128)} %rows_weigh.1.x_ref, f32[2,16,256]{2,1,0:T(8,128)} %get-tuple-element.27.p_ref, bf16[2,1024,512]{2,1,0:T(8,128)(2,1)} %constant.57.clone.w_ref, bf16[2,256,2048]{2,1,0:T(8,128)(2,1)} %constant.58.clone.v_ref), custom_call_target="tpu_custom_call" | custom-call | tf_op jit(solution)/shard_map/pupil_cols/pallas_call | solution.py:856
  182.6 24.6 %rows_back_band.1 = (f32[16,2,64,128]{3,2,1,0:T(8,128)}, f32[64,1024]{1,0:T(8,128)}) custom-call(f32[16,32,128]{2,1,0:T(8,128)} %pupil_cols.3.refs_0_, f32[2,64,1024]{2,1,0:T(8,128)} %get-tuple-element.25.refs_1_, f32[2,128,1024]{2,1,0:T(8,128)} %get-tuple-element.30.refs_2_, bf16[2,128,512]{2,1,0:T(8,128)(2,1)} %constant.53.clone.refs_1_.refs_3_, ...), custom_call_target="tpu_custom_call" | custom-call | tf_op jit(solution)/shard_map/rows_back_band/pallas_call | solution.py:686
  207.2 33.1 %cols.6.refs_0_ = f32[16,2,64,128]{3,2,1,0:T(8,128)} custom-call(f32[16,2,64,128]{3,2,1,0:T(8,128)} %get-tuple-element.31.x_ref, f32[2,2,4,256,128]{4,3,2,1,0:T(8,128)} %get-tuple-element.22.p_ref, bf16[2,512,256]{2,1,0:T(8,128)(2,1)} %constant.55.clone.w_ref, f32[2,3,256,128]{3,2,1,0:T(8,128)} %constant.56.clone.t_ref), custom_call_target="tpu_custom_call" | custom-call | tf_op jit(solution)/shard_map/cols/pallas_call | solution.py:794
  240.4 26.7 %rows_back.1 = (f32[16,2,64,128]{3,2,1,0:T(8,128)}, f32[64,1024]{1,0:T(8,128)}) custom-call(f32[16,2,64,128]{3,2,1,0:T(8,128)} %cols.6.refs_0_, f32[2,64,1024]{2,1,0:T(8,128)} %get-tuple-element.23.refs_1_, f32[2,128,1024]{2,1,0:T(8,128)} %get-tuple-element.32.refs_2_, bf16[2,512,512]{2,1,0:T(8,128)(2,1)} %constant.51.clone.refs_2_.refs_3_, ...), custom_call_target="tpu_custom_call" | custom-call | tf_op jit(solution)/shard_map/rows_back/pallas_call | solution.py:686
  267.0 22.9 %cols.7.refs_0_ = f32[16,1,64,128]{3,2,1,0:T(8,128)} custom-call(f32[16,2,64,128]{3,2,1,0:T(8,128)} %get-tuple-element.33.x_ref, f32[2,2,4,256,128]{4,3,2,1,0:T(8,128)} %get-tuple-element.22.p_ref, bf16[2,512,256]{2,1,0:T(8,128)(2,1)} %constant.55.clone.w_ref, f32[2,3,256,128]{3,2,1,0:T(8,128)} %constant.56.clone.t_ref), custom_call_target="tpu_custom_call" | custom-call | tf_op jit(solution)/shard_map/cols/pallas_call | solution.py:794
  289.9 3.6 %rows_leave.1 = f32[64,1024]{1,0:T(8,128)} custom-call(f32[16,1,64,128]{3,2,1,0:T(8,128)} %cols.7.refs_0_, f32[2,64,1024]{2,1,0:T(8,128)} %get-tuple-element.34.refs_1_, bf16[2,512,512]{2,1,0:T(8,128)(2,1)} %constant.51.clone.refs_2_.refs_3_, f32[8,256]{1,0:T(8,128)} %constant.54.clone.refs_4_.refs_2_.refs_5_.refs_3_), custom_call_target="tpu_custom_call" | custom-call | tf_op jit(solution)/shard_map/rows_leave/pallas_call | solution.py:686
  293.6 1.9 pad_maximum_fusion
  (12 shorter events, 0.2 us)
Async XLA Ops:
  289.9 3.6 %copy-start = (f32[64,1024]{1,0:T(8,128)S(1)}, f32[64,1024]{1,0:T(8,128)}, u32[]{:S(2)}) copy-start(f32[64,1024]{1,0:T(8,128)} %get-tuple-element.36) | copy-start | bytes 786436
  289.9 3.6 %copy-start.1 = (f32[64,1024]{1,0:T(8,128)S(1)}, f32[64,1024]{1,0:T(8,128)}, u32[]{:S(2)}) copy-start(f32[64,1024]{1,0:T(8,128)} %get-tuple-element.35) | copy-start | bytes 786436
